TPU v7x, 512 devices: a whole 4x4x16 slice. The times are simulated.
512 devices in a mesh: ctx: 16 (over z), exp: 32 (over x, y, core).
Axes of the slice: x: 4, y: 4, z: 16, core: 2. Of those that a mesh axis runs over, the one named last changes fastest.
Arguments:
- queries: bfloat16 [2048, 8192], P('ctx', 'exp'), may hold values from -6 to 6
- key_rows: bfloat16 [2048, 8192], P('ctx', 'exp'), may hold values from -6 to 6
- value_rows: bfloat16 [2048, 8192], P('ctx', 'exp'), may hold values from -6 to 6
- decay_rate: float32 [64], P('exp'), may hold values from 0.00024414062 to 0.04
- residual: bfloat16 [2048, 3072], P('exp', 'ctx'), may hold values from -6 to 6
- out_proj: bfloat16 [8192, 3072], P('exp', 'ctx'), may hold values from -0.0625 to 0.0625
- routes: int32 [2048, 2], P('exp'), may hold values from 0 to 15, all different within a row; in each aligned block of 64 rows (0 to 63, 64 to 127, ...) at most 16 rows name the same one
- gate_shares: int32 [2048, 2], P('exp'), may hold values from 1 to 8
- gate_proj: bfloat16 [32, 4096, 3072], P('exp', 'ctx'), may hold values from -0.109375 to 0.109375
- up_proj: bfloat16 [32, 4096, 3072], P('exp', 'ctx'), may hold values from -0.109375 to 0.109375
- down_proj: bfloat16 [32, 3072, 4096], P('exp', 'ctx'), may hold values from -0.0625 to 0.0625
Outputs:
- layer_out: bfloat16 [2048, 3072], P('exp', 'ctx')
Inputs may be any that keep to these rules, and one draw needn't show every extreme that they name: `routes`: each token names 2 different experts. Among the 64 tokens of each aligned block no expert is named by more than 16 tokens, a bound that some block reaches.
All inputs are finite; a program needn't handle non-finite values.
Results may differ from a plain program's by a relative error of at most 0.017.
Values may be sent and summed in bfloat16 or wider, within the bound.
A program may use at most 64 MiB of HBM per device.

v0:
```python
import jax
import jax.numpy as jnp
from jax import lax
from jax.sharding import PartitionSpec as P


def carried_in(shard, axis, combine, identity):
    peers, index = (lax.axis_size(axis), lax.axis_index(axis))
    everything = jax.tree.map(
        lambda part, kind: lax.all_gather(part.astype(kind), axis),
        shard,
        (jnp.bfloat16, jnp.bfloat16),
    )
    start = jax.tree.map(
        lambda part, zero: jnp.broadcast_to(jnp.asarray(zero, part.dtype), part.shape),
        shard,
        identity,
    )

    def step(k, before):
        reached = k < index
        new = combine(
            before, jax.tree.map(lambda part, own: part[k].astype(own.dtype), everything, shard)
        )
        return jax.tree.map(lambda a, b: jnp.where(reached, a, b), new, before)

    return lax.fori_loop(0, peers, step, start)


def rms_norm(vals):
    return vals * lax.rsqrt(jnp.mean(vals * vals, axis=-1, keepdims=True) + 1e-06)


def chain_combine(earlier, later):
    return (earlier[0] * later[0], later[0][:, None, None] * earlier[1] + later[1])


def body(
    queries,
    key_rows,
    value_rows,
    decay_rate,
    residual,
    out_proj,
    routes,
    gate_shares,
    gate_proj,
    up_proj,
    down_proj,
):
    count = queries.shape[0]
    heads = decay_rate.shape[0]
    width = queries.shape[1] // heads
    q_blk = queries.reshape(count, heads, width)
    k_blk = key_rows.reshape(count, heads, width)
    v_blk = value_rows.reshape(count, heads, width)
    places = jnp.arange(count, dtype=jnp.float32)
    lags = places[:, None] - places[None, :]
    inside = jnp.where(
        lags[None] >= 0, jnp.exp(-decay_rate[:, None, None] * jnp.maximum(lags, 0.0)[None]), 0.0
    )
    query_scale = jnp.exp(-decay_rate[:, None] * places[None, :]).T
    key_scale = jnp.exp(-decay_rate[:, None] * (count - places)[None, :]).T
    carry_scale = jnp.exp(-decay_rate * count)
    local = jnp.einsum(
        "shd,she->hde",
        k_blk.astype(jnp.float32) * key_scale[:, :, None],
        v_blk.astype(jnp.float32),
        precision=lax.Precision.HIGHEST,
    )
    identity = (jnp.ones((heads,), jnp.float32), jnp.zeros((heads, width, width), jnp.float32))
    earlier_state = carried_in((carry_scale, local), "ctx", chain_combine, identity)[1]
    scores = jnp.einsum("thd,shd->hts", q_blk, k_blk, preferred_element_type=jnp.float32)
    weight = (scores * inside).astype(jnp.bfloat16)
    intra = jnp.einsum("hts,shd->thd", weight, v_blk, preferred_element_type=jnp.float32)
    inter = (
        jnp.einsum(
            "thd,hde->the",
            q_blk.astype(jnp.float32),
            earlier_state,
            precision=lax.Precision.HIGHEST,
        )
        * query_scale[:, :, None]
    )
    attn = rms_norm(intra + inter).astype(jnp.bfloat16).reshape(count, heads * width)
    all_heads = lax.all_gather(attn, "ctx", axis=0, tiled=True)
    own_rows = all_heads.shape[0] // lax.axis_size("exp")
    summed = lax.psum_scatter(
        jnp.dot(all_heads, out_proj, preferred_element_type=jnp.float32).astype(jnp.bfloat16),
        "exp",
        scatter_dimension=0,
        tiled=True,
    ).astype(jnp.float32)
    stream = (summed + residual.astype(jnp.float32)).astype(jnp.bfloat16)
    holders = lax.axis_size("exp")
    experts = holders // 2
    tops = routes.shape[1]
    capacity = 2 * own_rows * tops // experts
    flat = routes.reshape(-1)
    marks = (flat[:, None] == jnp.arange(experts, dtype=jnp.int32)[None, :]).astype(jnp.int32)
    before = jnp.cumsum(marks, axis=0) - marks
    slot = jnp.sum(marks * before, axis=1)
    target = flat * capacity + slot
    placed = (target[:, None] == jnp.arange(experts * capacity, dtype=jnp.int32)[None, :]).reshape(
        own_rows, tops, experts * capacity
    )
    picker = jnp.any(placed, axis=1).astype(jnp.bfloat16)
    shares = gate_shares.astype(jnp.float32)
    shares = shares / jnp.sum(shares, axis=1, keepdims=True)
    combiner = jnp.sum(placed.astype(jnp.float32) * shares[:, :, None], axis=1)
    pick_dims = (((0,), (0,)), ((), ()))
    contract = (((1,), (1,)), ((), ()))
    whole = lax.all_gather(stream, "ctx", axis=1, tiled=True)
    normed = rms_norm(whole.astype(jnp.float32)).astype(jnp.bfloat16)
    outgoing = lax.dot_general(
        picker, normed, pick_dims, preferred_element_type=jnp.float32
    ).astype(jnp.bfloat16)
    feats = outgoing.shape[1]
    shaped = outgoing.reshape(experts, 1, capacity, feats)
    arrived = lax.all_to_all(
        jnp.broadcast_to(shaped, (experts, 2, capacity, feats)).reshape(holders, capacity, feats),
        "exp",
        split_axis=0,
        concat_axis=0,
        tiled=True,
    )
    inputs = arrived.reshape(holders * capacity, -1)
    gate = lax.dot_general(inputs, gate_proj[0], contract, preferred_element_type=jnp.float32)
    upper = lax.dot_general(inputs, up_proj[0], contract, preferred_element_type=jnp.float32)
    hidden = (jax.nn.silu(gate) * upper).astype(jnp.bfloat16)
    down_local = down_proj[0]
    produced = lax.dot_general(
        lax.all_gather(hidden, "ctx", axis=1, tiled=True),
        down_local,
        contract,
        preferred_element_type=jnp.float32,
    )
    leaving = produced.reshape(holders, capacity, -1)
    homecoming = lax.all_to_all(
        leaving.astype(jnp.bfloat16), "exp", split_axis=0, concat_axis=0, tiled=True
    ).astype(leaving.dtype)
    feats = homecoming.shape[2]
    halves = homecoming.reshape(experts, 2, capacity, feats)
    expert_out = (
        (halves[:, 0] + halves[:, 1]).astype(jnp.bfloat16).reshape(experts * capacity, feats)
    )
    mixed = jnp.dot(combiner, expert_out.astype(jnp.float32), precision=lax.Precision.HIGHEST)
    return (stream.astype(jnp.float32) + mixed).astype(jnp.bfloat16)


def solution(mesh):
    in_specs = (
        P("ctx", "exp"),
        P("ctx", "exp"),
        P("ctx", "exp"),
        P("exp"),
        P("exp", "ctx"),
        P("exp", "ctx"),
        P("exp", None),
        P("exp", None),
        P("exp", "ctx", None),
        P("exp", "ctx", None),
        P("exp", "ctx", None),
    )
    out_specs = P("exp", "ctx")
    return jax.shard_map(body, mesh=mesh, in_specs=in_specs, out_specs=out_specs, check_vma=False)
```

profile of v0, /device:TPU:1, one launch (start us, length us, event | category | flops | bytes accessed | tf_op | source)
XLA Modules:
  0.0 476.2 jit_solution(14987146697608298980)
XLA Ops:
  7.4 1.0 copy.66
  8.4 1.7 convolution_convert_fusion.2
  10.2 1.3 dynamic-slice
  12.4 31.5 %all-reduce = bf16[32]{0:T(256)(128)(2,1)S(1)} all-reduce(bf16[32]{0:T(256)(128)(2,1)S(1)} %dynamic-update-slice), channel_id=2, replica_groups=mesh['ctx'=16,'exp'=32] {'ctx'}, use_global_device_ids=true, to_apply=%add | all-reduce | flops 32 | bytes 128
  44.1 33.1 %all-gather.11.cloned.1.call-done = bf16[32,128,128]{2,1,0:T(8,128)(2,1)} async-done(((bf16[2,128,128]{2,1,0:T(8,128)(2,1)}), bf16[32,128,128]{2,1,0:T(8,128)(2,1)}) %all-gather.11.cloned.1.call-update) | async-done | bytes 1048592 | tf_op jit(solution)/shard_map/all_gather | solution.py:10
  77.1 15.5 %while.14 = (s32[]{:T(128)}, f32[2,128,128]{2,1,0:T(8,128)S(1)}, s32[]{:T(128)}, bf16[16,2]{1,0:T(8,128)(2,1)S(1)}, bf16[16,2,128,128]{3,2,1,0:T(8,128)(2,1)}, /*index=5*/s32[]{:T(128)}, s32[]{:T(128)}) while((s32[]{:T(128)}, f32[2,128,128]{2,1,0:T(8,128)S(1)}, s32[]{:T(128)}, bf16[16,2]{1,0:T(8,128)(2,1)S(1)}, ...), condition=%wide.region_1.2_spmd.clone, body=%wide.region_0.1_spmd.clone.sunk | while | flops 163846 | bytes 327805 | solution.py:27
  78.1 0.9 fusion.66
  79.1 0.9 fusion.66
  80.1 0.9 fusion.66
  81.0 0.9 fusion.66
  82.0 0.9 fusion.66
  83.0 0.9 fusion.66
  83.9 0.9 fusion.66
  94.1 67.7 %all-gather.7.cloned.1.call-done = bf16[2048,256]{0,1:T(8,128)(2,1)} async-done(((bf16[128,256]{0,1:T(8,128)(2,1)}), bf16[2048,256]{0,1:T(8,128)(2,1)}) %all-gather.7.cloned.1.call-update) | async-done | bytes 1048592 | tf_op jit(solution)/shard_map/all_gather | solution.py:86
  161.8 2.7 convolution_convert_fusion.1
  165.6 106.5 %reduce-scatter.2.cloned.1.call-done = bf16[64,192]{1,0:T(8,128)(2,1)} async-done(((bf16[2048,192]{1,0:T(8,128)(2,1)}), bf16[64,192]{1,0:T(8,128)(2,1)}) %reduce-scatter.2.cloned.1.call-update) | async-done | bytes 24592 | tf_op jit(solution)/shard_map/reduce_scatter | solution.py:88
  272.9 26.8 %all-gather.2 = bf16[16,192,64]{1,2,0:T(8,128)(2,1)S(1)} all-gather(bf16[1,192,64]{1,2,0:T(8,128)(2,1)S(1)} %fusion.46), channel_id=1, replica_groups=mesh['ctx'=16,'exp'=32] {'ctx'}, dimensions={0}, use_global_device_ids=true | all-gather | bytes 417792 | tf_op jit(solution)/shard_map/all_gather | solution.py:113
  301.6 52.9 %all_to_all.10 = bf16[32,16,3072]{2,1,0:T(8,128)(2,1)S(1)} all-to-all(bf16[32,16,3072]{2,1,0:T(8,128)(2,1)S(1)} %bitcast.91), channel_id=1, replica_groups=mesh['ctx'=16,'exp'=32] {'exp'}, dimensions={0} | all-to-all | bytes 6291456 | tf_op jit(solution)/shard_map/all_to_all | solution.py:120
  354.5 1.0 fusion.5
  355.9 1.7 fusion.10
  357.7 79.8 %all-gather.9.cloned.1.call-done = bf16[512,4096]{1,0:T(8,128)(2,1)} async-done(((bf16[512,256]{1,0:T(8,128)(2,1)}), bf16[512,4096]{1,0:T(8,128)(2,1)}) %all-gather.9.cloned.1.call-update) | async-done | bytes 4194320 | tf_op jit(solution)/shard_map/all_gather | solution.py:133
  437.5 4.2 fusion.13
  441.7 18.0 %all-to-all-start.1 = ((bf16[32,16,192]{2,1,0:T(8,128)(2,1)}), bf16[32,16,192]{2,1,0:T(8,128)(2,1)S(1)}, u32[]{:S(2)}, u32[]{:S(2)}) async-start(bf16[32,16,192]{2,1,0:T(8,128)(2,1)} %fusion.13), calls=%async_computation.2 | async-start | bytes 524288 | tf_op jit(solution)/shard_map/all_to_all | solution.py:139
  459.8 8.9 %all-to-all-done.1 = bf16[32,16,192]{2,1,0:T(8,128)(2,1)S(1)} async-done(((bf16[32,16,192]{2,1,0:T(8,128)(2,1)}), bf16[32,16,192]{2,1,0:T(8,128)(2,1)S(1)}, u32[]{:S(2)}, u32[]{:S(2)}) %all-to-all-start.1) | async-done | bytes 196640 | tf_op jit(solution)/shard_map/all_to_all | solution.py:139
  (88 shorter events, 16.4 us)
Async XLA Ops:
  6.5 348.0 %copy-start = (bf16[1,256,3072]{2,1,0:T(8,128)(2,1)S(1)}, bf16[1,256,3072]{2,1,0:T(8,128)(2,1)}, u32[]{:S(2)}) copy-start(bf16[1,256,3072]{2,1,0:T(8,128)(2,1)} %param.21) | copy-start | bytes 4718596
  6.5 86.4 %copy-start.1 = (bf16[128,256]{1,0:T(8,128)(2,1)S(1)}, bf16[128,256]{1,0:T(8,128)(2,1)}, u32[]{:S(2)}) copy-start(bf16[128,256]{1,0:T(8,128)(2,1)} %param.15) | copy-start | bytes 196612
  6.5 86.1 %copy-start.2 = (bf16[128,256]{1,0:T(8,128)(2,1)S(1)}, bf16[128,256]{1,0:T(8,128)(2,1)}, u32[]{:S(2)}) copy-start(bf16[128,256]{1,0:T(8,128)(2,1)} %param.13) | copy-start | bytes 196612
  6.5 155.2 %copy-start.5 = (bf16[256,192]{0,1:T(8,128)(2,1)S(1)}, bf16[256,192]{0,1:T(8,128)(2,1)}, u32[]{:S(2)}) copy-start(bf16[256,192]{0,1:T(8,128)(2,1)} %param.18) | copy-start | bytes 294916
  6.5 70.6 %all-gather.11.cloned.1.call-start = ((), (), s32[]{:S(2)}) async-start(), calls=%async_computation.6 | async-start | bytes 1114112 | tf_op jit(solution)/shard_map/all_gather | solution.py:10
  10.1 151.6 %all-gather.7.cloned.1.call-start = ((), (), s32[]{:S(2)}) async-start(), calls=%async_computation.3 | async-start | bytes 1114112 | tf_op jit(solution)/shard_map/all_gather | solution.py:86
  93.0 71.6 %copy-start.6 = (s32[64,2]{0,1:T(2,128)S(1)}, s32[64,2]{0,1:T(2,128)}, u32[]{:S(2)}) copy-start(s32[64,2]{0,1:T(2,128)} %param.19) | copy-start | bytes 1540
  93.3 178.8 %copy-start.3 = (bf16[64,192]{1,0:T(8,128)(2,1)S(1)}, bf16[64,192]{1,0:T(8,128)(2,1)}, u32[]{:S(2)}) copy-start(bf16[64,192]{1,0:T(8,128)(2,1)} %param.17) | copy-start | bytes 73732
  94.0 178.1 %reduce-scatter.2.cloned.1.call-start = ((), (), s32[]{:S(2)}) async-start(), calls=%async_computation.4 | async-start | bytes 1081344 | tf_op jit(solution)/shard_map/reduce_scatter | solution.py:88
  164.5 273.0 %all-gather.9.cloned.1.call-start = ((), (), s32[]{:S(2)}) async-start(), calls=%async_computation.5 | async-start | bytes 4456448 | tf_op jit(solution)/shard_map/all_gather | solution.py:133
  354.5 1.4 copy-start.8
  355.9 1.7 copy-start.7
  355.9 81.6 %copy-start.9 = (bf16[1,192,4096]{2,1,0:T(8,128)(2,1)S(1)}, bf16[1,192,4096]{2,1,0:T(8,128)(2,1)}, u32[]{:S(2)}) copy-start(bf16[1,192,4096]{2,1,0:T(8,128)(2,1)} %param.23) | copy-start | bytes 4718596
  437.5 31.3 %copy-start.4 = (bf16[64,192]{1,0:T(8,128)(2,1)S(1)}, bf16[64,192]{1,0:T(8,128)(2,1)}, u32[]{:S(2)}) copy-start(bf16[64,192]{1,0:T(8,128)(2,1)} %reduce-scatter.2.cloned.1.call-done) | copy-start | bytes 73732
  441.7 27.0 %all-to-all-start.1 = ((bf16[32,16,192]{2,1,0:T(8,128)(2,1)}), bf16[32,16,192]{2,1,0:T(8,128)(2,1)S(1)}, u32[]{:S(2)}, u32[]{:S(2)}) async-start(bf16[32,16,192]{2,1,0:T(8,128)(2,1)} %fusion.13), calls=%async_computation.2 | async-start | bytes 524288 | tf_op jit(solution)/shard_map/all_to_all | solution.py:139
Sparse Core Ops, SparseCore 0:
  10.2 66.8 all-gather.10
  94.1 67.5 all-gather.6
  166.1 105.9 reduce-scatter.1
  357.8 79.7 all-gather.8
where the time goes:
time: 477 us; the launch traced here: 476 us
  waiting for transfers between devices  296 us (62%)
  blocking collectives  111 us (23%)
  other arithmetic  18.3 us (4%)
  starting transfers between devices  18.2 us (4%)
  between operations  14 us (3%)
  matrix products  13.4 us (3%)
    reduce_scatter x1, waiting for transfers between devices, body(): lax.psum_scatter(jnp.dot(all_heads, out_proj, preferred_element_type=jnp....  107 us
    all_gather x1, waiting for transfers between devices, body(): lax.all_gather(hidden, 'ctx', axis=1, tiled=True)  79.8 us
    all_gather x1, waiting for transfers between devices, body(): all_heads = lax.all_gather(attn, 'ctx', axis=0, tiled=True)  67.7 us
    all_to_all x1, blocking collectives, body(): lax.all_to_all(jnp.broadcast_to(shaped, (experts, 2, capacity, feats)).re...  52.9 us
    all_gather x1, waiting for transfers between devices, carried_in(): lax.all_gather(part.astype(kind), axis)  33.1 us
    unnamed x1, blocking collectives  31.5 us
    all_gather x1, blocking collectives, body(): whole = lax.all_gather(stream, 'ctx', axis=1, tiled=True)  26.8 us
    all_to_all x1, starting transfers between devices, body(): lax.all_to_all(leaving.astype(jnp.bfloat16), 'exp', split_axis=0, concat_...  18 us
  transfers between devices with their start and end apart: 5, of which 5 were waited for; matrix products, arithmetic and copies ran while one was open for 1% of the time, Pallas kernels for 0%

commit v1 on v0

v1 whole, which is shorter than its diff:
```python
import functools
import jax
import jax.numpy as jnp
from jax import lax
from jax.experimental import pallas as pl
from jax.experimental.pallas import tpu as pltpu
from jax.sharding import PartitionSpec as P

MESH = pl.DeviceIdType.MESH


def ring_kernel(n, chunks, paired, x_ref, out_ref, send, recv, own_sem, pass_send, pass_recv):
    me = lax.axis_index("ctx")
    col = lax.axis_index("exp")
    near = (lax.rem(me + 1, n), lax.rem(me + n - 1, n))
    core = lax.rem(col, 2)
    partner = col + 1 - 2 * core
    half = n // 2

    barrier = pltpu.get_barrier_semaphore()
    for peer in near:
        pl.semaphore_signal(barrier, inc=1, device_id={"ctx": peer}, device_id_type=MESH)
    if paired:
        pl.semaphore_signal(barrier, inc=1, device_id={"exp": partner}, device_id_type=MESH)
    keep = pltpu.make_async_copy(x_ref, out_ref.at[me], own_sem)
    keep.start()
    pl.semaphore_wait(barrier, 3 if paired else 2)

    def origin_of(way, step):
        return lax.rem(me - step + n, n) if way == 0 else lax.rem(me + step, n)

    def place(ref, index, chunk, side):
        lead = () if index is None else (index,)
        return ref.at[lead + ((side, chunk) if paired else (chunk,))]

    def hop(way, step, chunk):
        origin = origin_of(way, step)
        src = place(x_ref, None, chunk, core) if step == 0 else place(out_ref, origin, chunk, core)
        return pltpu.make_async_remote_copy(
            src_ref=src,
            dst_ref=place(out_ref, origin, chunk, core),
            send_sem=send.at[way, step, chunk],
            recv_sem=recv.at[way, step, chunk],
            device_id={"ctx": near[way]},
            device_id_type=MESH,
        )

    def landed(way, step, chunk):
        spot = place(out_ref, origin_of(way, step + 1), chunk, core)
        return pltpu.make_async_remote_copy(
            src_ref=spot,
            dst_ref=spot,
            send_sem=send.at[way, step, chunk],
            recv_sem=recv.at[way, step, chunk],
            device_id={"ctx": near[way]},
            device_id_type=MESH,
        )

    def across(way, step, chunk, side):
        spot = place(out_ref, origin_of(way, step + 1), chunk, side)
        return pltpu.make_async_remote_copy(
            src_ref=spot,
            dst_ref=spot,
            send_sem=pass_send.at[way, step, chunk],
            recv_sem=pass_recv.at[way, step, chunk],
            device_id={"exp": partner},
            device_id_type=MESH,
        )

    def carried(way, step, chunk):
        return step < half - 1 or (chunk < chunks // 2) == (way == 0)

    order = [(step, chunk, way) for step in range(half) for chunk in range(chunks) for way in range(2)]
    moved = [(way, step, chunk) for step, chunk, way in order if carried(way, step, chunk)]
    for step in range(half + 1):
        for chunk in range(chunks):
            for way in range(2):
                if step > 0 and carried(way, step - 1, chunk):
                    landed(way, step - 1, chunk).wait_recv()
                if step < half and carried(way, step, chunk):
                    hop(way, step, chunk).start()
                if paired and step > 0 and carried(way, step - 1, chunk):
                    across(way, step - 1, chunk, core).start()
    for item in moved:
        hop(*item).wait_send()
    if paired:
        for item in moved:
            across(*item, core).wait_send()
            across(*item, 1 - core).wait_recv()
    keep.wait()


def ring_gather(x, ident, paired=False):
    n = lax.axis_size("ctx")
    chunks = x.shape[1] if paired else x.shape[0]
    sems = pltpu.SemaphoreType.DMA((2, n // 2, chunks))
    return pl.pallas_call(
        functools.partial(ring_kernel, n, chunks, paired),
        out_shape=jax.ShapeDtypeStruct((n,) + x.shape, x.dtype),
        in_specs=[pl.BlockSpec(memory_space=pltpu.VMEM)],
        out_specs=pl.BlockSpec(memory_space=pltpu.VMEM),
        scratch_shapes=[sems, sems, pltpu.SemaphoreType.DMA, sems, sems],
        compiler_params=pltpu.CompilerParams(collective_id=ident, has_side_effects=True),
        name="ring_gather",
    )(x)


def exchange_kernel(n, share, x_ref, out_ref, send, recv, own_sem):
    me = lax.axis_index("exp")
    barrier = pltpu.get_barrier_semaphore()

    def greet(j, carry):
        pl.semaphore_signal(
            barrier, inc=1, device_id={"exp": lax.rem(me + j, n)}, device_id_type=MESH
        )
        return carry

    lax.fori_loop(1, n, greet, 0)
    keep = pltpu.make_async_copy(x_ref.at[me // share], out_ref.at[me], own_sem)
    keep.start()
    pl.semaphore_wait(barrier, n - 1)

    def outward(j):
        peer = lax.rem(me + j, n)
        return pltpu.make_async_remote_copy(
            src_ref=x_ref.at[peer // share],
            dst_ref=out_ref.at[me],
            send_sem=send.at[j],
            recv_sem=recv.at[j],
            device_id={"exp": peer},
            device_id_type=MESH,
        )

    def inward(j):
        spot = out_ref.at[lax.rem(me - j + n, n)]
        return pltpu.make_async_remote_copy(
            src_ref=spot,
            dst_ref=spot,
            send_sem=send.at[j],
            recv_sem=recv.at[j],
            device_id={"exp": lax.rem(me + j, n)},
            device_id_type=MESH,
        )

    def launch(j, carry):
        outward(j).start()
        return carry

    def finish(j, carry):
        inward(j).wait_recv()
        outward(j).wait_send()
        return carry

    lax.fori_loop(1, n, launch, 0)
    lax.fori_loop(1, n, finish, 0)
    keep.wait()


def exchange(x, ident):
    n = lax.axis_size("exp")
    sems = pltpu.SemaphoreType.DMA((n,))
    return pl.pallas_call(
        functools.partial(exchange_kernel, n, n // x.shape[0]),
        out_shape=jax.ShapeDtypeStruct((n,) + x.shape[1:], x.dtype),
        in_specs=[pl.BlockSpec(memory_space=pltpu.VMEM)],
        out_specs=pl.BlockSpec(memory_space=pltpu.VMEM),
        scratch_shapes=[sems, sems, pltpu.SemaphoreType.DMA],
        compiler_params=pltpu.CompilerParams(collective_id=ident, has_side_effects=True),
        name="exchange",
    )(x)


def rms_norm(vals, axis):
    return vals * lax.rsqrt(jnp.mean(vals * vals, axis=axis, keepdims=True) + 1e-06)


def body(
    queries,
    key_rows,
    value_rows,
    decay_rate,
    residual,
    out_proj,
    routes,
    gate_shares,
    gate_proj,
    up_proj,
    down_proj,
):
    count = queries.shape[0]
    heads = decay_rate.shape[0]
    width = queries.shape[1] // heads
    ring = lax.axis_size("ctx")
    index = lax.axis_index("ctx")
    q_blk = queries.reshape(count, heads, width)
    k_blk = key_rows.reshape(count, heads, width)
    v_blk = value_rows.reshape(count, heads, width)
    places = jnp.arange(count, dtype=jnp.float32)
    lags = places[:, None] - places[None, :]
    inside = jnp.where(
        lags[None] >= 0, jnp.exp(-decay_rate[:, None, None] * jnp.maximum(lags, 0.0)[None]), 0.0
    )
    query_scale = jnp.exp(-decay_rate[:, None] * places[None, :]).T
    key_scale = jnp.exp(-decay_rate[:, None] * (count - places)[None, :]).T
    local = jnp.einsum(
        "shd,she->hde",
        k_blk.astype(jnp.float32) * key_scale[:, :, None],
        v_blk.astype(jnp.float32),
        precision=lax.Precision.HIGHEST,
    ).astype(jnp.bfloat16)
    states = ring_gather(local.reshape(4, heads * width // 4, width), 0)
    states = states.reshape(ring, heads, width, width).astype(jnp.float32)
    between = index - 1 - jnp.arange(ring)
    fade = jnp.where(
        between[:, None] >= 0,
        jnp.exp(
            -decay_rate[None, :] * count * jnp.maximum(between, 0)[:, None].astype(jnp.float32)
        ),
        0.0,
    )
    earlier_state = jnp.sum(fade[:, :, None, None] * states, axis=0)
    scores = jnp.einsum("thd,shd->hts", q_blk, k_blk, preferred_element_type=jnp.float32)
    weight = (scores * inside).astype(jnp.bfloat16)
    intra = jnp.einsum("hts,shd->thd", weight, v_blk, preferred_element_type=jnp.float32)
    inter = (
        jnp.einsum(
            "thd,hde->the",
            q_blk.astype(jnp.float32),
            earlier_state,
            precision=lax.Precision.HIGHEST,
        )
        * query_scale[:, :, None]
    )
    attn = rms_norm(intra + inter, -1).astype(jnp.bfloat16).reshape(4, count // 4, heads * width)
    all_heads = ring_gather(attn, 1).reshape(ring * count, heads * width)

    holders = lax.axis_size("exp")
    experts = holders // 2
    own_rows, slice_width = residual.shape
    partial = jnp.dot(all_heads, out_proj, preferred_element_type=jnp.float32).astype(jnp.bfloat16)
    parts = exchange(partial.reshape(holders, own_rows, slice_width), 2)
    summed = jnp.sum(parts.astype(jnp.float32), axis=0)
    stream = (summed + residual.astype(jnp.float32)).astype(jnp.bfloat16)

    tops = routes.shape[1]
    capacity = 2 * own_rows * tops // experts
    flat = routes.reshape(-1)
    marks = (flat[:, None] == jnp.arange(experts, dtype=jnp.int32)[None, :]).astype(jnp.int32)
    before = jnp.cumsum(marks, axis=0) - marks
    slot = jnp.sum(marks * before, axis=1)
    target = flat * capacity + slot
    placed = (target[:, None] == jnp.arange(experts * capacity, dtype=jnp.int32)[None, :]).reshape(
        own_rows, tops, experts * capacity
    )
    picker = jnp.any(placed, axis=1).astype(jnp.bfloat16)
    shares = gate_shares.astype(jnp.float32)
    shares = shares / jnp.sum(shares, axis=1, keepdims=True)
    combiner = jnp.sum(placed.astype(jnp.float32) * shares[:, :, None], axis=1)

    outgoing = lax.dot_general(
        picker, stream, (((0,), (0,)), ((), ())), preferred_element_type=jnp.float32
    ).astype(jnp.bfloat16)
    arrived = exchange(outgoing.reshape(experts, capacity, slice_width), 3)
    slots = holders * capacity
    turned = arrived.reshape(slots, slice_width).T.reshape(2, 2, slice_width // 4, slots)
    tokens = ring_gather(turned, 4, paired=True).reshape(ring * slice_width, slots)
    normed = rms_norm(tokens.astype(jnp.float32), 0).astype(jnp.bfloat16)
    gate = jnp.dot(gate_proj[0], normed, preferred_element_type=jnp.float32)
    upper = jnp.dot(up_proj[0], normed, preferred_element_type=jnp.float32)
    hidden = (jax.nn.silu(gate) * upper).astype(jnp.bfloat16)
    units = hidden.shape[0]
    whole = ring_gather(hidden.reshape(4, units // 4, slots), 5).reshape(ring * units, slots)
    produced = lax.dot_general(
        whole, down_proj[0], (((0,), (1,)), ((), ())), preferred_element_type=jnp.float32
    ).astype(jnp.bfloat16)
    homecoming = exchange(produced.reshape(holders, capacity, slice_width), 6)
    halves = homecoming.astype(jnp.float32).reshape(experts, 2, capacity, slice_width)
    expert_out = (
        (halves[:, 0] + halves[:, 1]).astype(jnp.bfloat16).reshape(experts * capacity, slice_width)
    )
    mixed = jnp.dot(combiner, expert_out.astype(jnp.float32), precision=lax.Precision.HIGHEST)
    return (stream.astype(jnp.float32) + mixed).astype(jnp.bfloat16)


def solution(mesh):
    in_specs = (
        P("ctx", "exp"),
        P("ctx", "exp"),
        P("ctx", "exp"),
        P("exp"),
        P("exp", "ctx"),
        P("exp", "ctx"),
        P("exp", None),
        P("exp", None),
        P("exp", "ctx", None),
        P("exp", "ctx", None),
        P("exp", "ctx", None),
    )
    out_specs = P("exp", "ctx")
    return jax.shard_map(body, mesh=mesh, in_specs=in_specs, out_specs=out_specs, check_vma=False)
```

time: 477 us -> 247 us (0.52)
  waiting for transfers between devices: 296 us -> 0 us
  Pallas kernels: 0 us -> 216 us
  blocking collectives: 111 us -> 0 us
  starting transfers between devices: 18.2 us -> 0 us
  between operations: 14 us -> 0.33 us
  other arithmetic: 18.3 us -> 9.27 us
    pallas_call x0 -> x7, Pallas kernels: none -> 216 us  [the longest x4 150 us: ring_gather(): pl.pallas_call(functools.partial(ring_kernel, n, chunks, paired), out_sha...]
    all_gather x3 -> x0, waiting for transfers between devices: 181 us -> none  [the longest x1 79.8 us: body(): lax.all_gather(hidden, 'ctx', axis=1, tiled=True)]
    reduce_scatter x1 -> x0, waiting for transfers between devices: 107 us -> none  [body(): lax.psum_scatter(jnp.dot(all_heads, out_proj, preferred_element_type=jnp....]
    all_to_all x1 -> x0, blocking collectives: 52.9 us -> none  [body(): lax.all_to_all(jnp.broadcast_to(shaped, (experts, 2, capacity, feats)).re...]
    unnamed x1 -> x0, blocking collectives: 31.5 us -> none
    all_gather x1 -> x0, blocking collectives: 26.8 us -> none  [body(): whole = lax.all_gather(stream, 'ctx', axis=1, tiled=True)]
    all_to_all x1 -> x0, starting transfers between devices: 18 us -> none  [body(): lax.all_to_all(leaving.astype(jnp.bfloat16), 'exp', split_axis=0, concat_...]
    select_n x16 -> x1, other arithmetic: 14.9 us -> 0.07 us  [body(): jnp.where(between[:, None] >= 0, jnp.exp(-decay_rate[None, :] * count * j...]
  transfers between devices with their start and end apart: 5 -> 0, of which waited for: 5 -> 0; matrix products, arithmetic and copies ran while one was open for 1% -> 0% of each run, Pallas kernels for 0% -> 0%
where the time goes in v1:
time: 247 us; the launch traced here: 246 us
  Pallas kernels  216 us (87%)
  matrix products  12.7 us (5%)
  other arithmetic  9.27 us (4%)
  local copies, waits for them, and re-layouts  7.43 us (3%)
    pallas_call x4, Pallas kernels, ring_gather(): pl.pallas_call(functools.partial(ring_kernel, n, chunks, paired), out_sha...  150 us
    pallas_call x3, Pallas kernels, exchange(): pl.pallas_call(functools.partial(exchange_kernel, n, n // x.shape[0]), ou...  65.7 us

profile of v1, /device:TPU:1, one launch (start us, length us, event | category | flops | bytes accessed | tf_op | source)
XLA Modules:
  0.0 245.6 jit_solution(1336747197686352673)
XLA Ops:
  0.9 1.0 copy.74
  1.8 1.7 convolution_convert_fusion.2
  3.5 34.5 %ring_gather.4 = bf16[16,4,64,128]{3,2,1,0:T(8,128)(2,1)} custom-call(bf16[4,64,128]{2,1,0:T(8,128)(2,1)} %bitcast.108), custom_call_target="tpu_custom_call" | custom-call | tf_op jit(solution)/shard_map/ring_gather/pallas_call | solution.py:97
  38.2 1.5 multiply_reduce_fusion
  39.8 1.1 fusion.23
  41.0 1.2 multiply_reduce_fusion.1
  43.0 26.7 %ring_gather.5 = bf16[16,4,32,256]{3,2,1,0:T(8,128)(2,1)} custom-call(bf16[4,32,256]{2,1,0:T(8,128)(2,1)} %reshape.237.x_ref), custom_call_target="tpu_custom_call" | custom-call | tf_op jit(solution)/shard_map/ring_gather/pallas_call | solution.py:97
  69.8 1.7 convolution_convert_fusion
  71.5 1.3 copy.67
  72.8 36.2 %exchange.3 = bf16[32,64,192]{2,1,0:T(8,128)(2,1)} custom-call(bf16[32,64,192]{2,1,0:T(8,128)(2,1)} %bitcast.93), custom_call_target="tpu_custom_call" | custom-call | tf_op jit(solution)/shard_map/exchange/pallas_call | solution.py:162
  109.0 1.4 convert_reduce_fusion
  112.5 15.4 %exchange.4 = bf16[32,16,192]{2,1,0:T(8,128)(2,1)} custom-call(bf16[16,16,192]{2,1,0:T(8,128)(2,1)} %bitcast.104), custom_call_target="tpu_custom_call" | custom-call | tf_op jit(solution)/shard_map/exchange/pallas_call | solution.py:162
  127.9 1.8 copy.71
  129.7 36.9 %ring_gather.6 = bf16[16,2,2,48,512]{4,3,2,1,0:T(8,128)(2,1)} custom-call(bf16[2,2,48,512]{3,2,1,0:T(8,128)(2,1)} %bitcast.101), custom_call_target="tpu_custom_call" | custom-call | tf_op jit(solution)/shard_map/ring_gather/pallas_call | solution.py:97
  166.6 2.8 %fusion = f32[512]{0:T(512)S(1)} fusion(bf16[16,2,2,48,512]{4,3,2,1,0:T(8,128)(2,1)} %ring_gather.6), kind=kLoop, calls=%fused_computation.2 | loop fusion | flops 4718080 | bytes 3147776 | tf_op jit(solution)/shard_map/reduce_sum | solution.py:174
  169.4 0.8 fusion.1
  170.3 1.0 fusion.8
  171.7 1.7 fusion.17
  173.4 52.1 %ring_gather.7 = bf16[16,4,64,512]{3,2,1,0:T(8,128)(2,1)} custom-call(bf16[4,64,512]{2,1,0:T(8,128)(2,1)} %bitcast.107), custom_call_target="tpu_custom_call" | custom-call | tf_op jit(solution)/shard_map/ring_gather/pallas_call | solution.py:97
  225.5 3.2 %fusion.20 = bf16[512,192]{0,1:T(8,128)(2,1)S(1)} fusion(bf16[4096,512]{1,0:T(8,128)(2,1)} %bitcast.94, bf16[1,192,4096]{2,1,0:T(8,128)(2,1)S(1)} %copy-done.7), kind=kOutput, calls=%fused_computation.17 | convolution fusion | flops 805404672 | bytes 5963776 | tf_op jit(solution)/shard_map/dot_general | solution.py:273
  228.7 0.8 copy.72
  229.5 14.1 %exchange.5 = bf16[32,16,192]{2,1,0:T(8,128)(2,1)} custom-call(bf16[32,16,192]{2,1,0:T(8,128)(2,1)} %bitcast.100), custom_call_target="tpu_custom_call" | custom-call | tf_op jit(solution)/shard_map/exchange/pallas_call | solution.py:162
  243.6 1.0 convert.1
  244.8 0.8 fusion.26
  (46 shorter events, 4.6 us)
Async XLA Ops:
  0.0 170.3 %copy-start = (bf16[1,256,3072]{2,1,0:T(8,128)(2,1)S(1)}, bf16[1,256,3072]{2,1,0:T(8,128)(2,1)}, u32[]{:S(2)}) copy-start(bf16[1,256,3072]{2,1,0:T(8,128)(2,1)} %param.19) | copy-start | bytes 4718596
  0.0 69.7 %copy-start.3 = (bf16[256,192]{0,1:T(8,128)(2,1)S(1)}, bf16[256,192]{0,1:T(8,128)(2,1)}, u32[]{:S(2)}) copy-start(bf16[256,192]{0,1:T(8,128)(2,1)} %param.16) | copy-start | bytes 294916
  69.8 40.7 %copy-start.4 = (s32[64,2]{0,1:T(2,128)S(1)}, s32[64,2]{0,1:T(2,128)}, u32[]{:S(2)}) copy-start(s32[64,2]{0,1:T(2,128)} %param.17) | copy-start | bytes 1540
  71.5 39.9 %copy-start.2 = (bf16[64,192]{1,0:T(8,128)(2,1)S(1)}, bf16[64,192]{1,0:T(8,128)(2,1)}, u32[]{:S(2)}) copy-start(bf16[64,192]{1,0:T(8,128)(2,1)} %param.15) | copy-start | bytes 73732
  166.6 2.8 %copy-start.1 = (bf16[16,2,2,48,512]{4,3,2,1,0:T(8,128)(2,1)S(1)}, bf16[16,2,2,48,512]{4,3,2,1,0:T(8,128)(2,1)}, u32[]{:S(2)}) copy-start(bf16[16,2,2,48,512]{4,3,2,1,0:T(8,128)(2,1)} %ring_gather.6) | copy-start | bytes 9437188
  170.2 1.4 copy-start.6
  173.4 52.1 %copy-start.7 = (bf16[1,192,4096]{2,1,0:T(8,128)(2,1)S(1)}, bf16[1,192,4096]{2,1,0:T(8,128)(2,1)}, u32[]{:S(2)}) copy-start(bf16[1,192,4096]{2,1,0:T(8,128)(2,1)} %param.21) | copy-start | bytes 4718596
  225.5 19.2 %copy-start.5 = (s32[64,2]{0,1:T(2,128)S(1)}, s32[64,2]{0,1:T(2,128)}, u32[]{:S(2)}) copy-start(s32[64,2]{0,1:T(2,128)} %param.18) | copy-start | bytes 1540

commit v2 on v0

v2 whole, which is shorter than its diff:
```python
import functools
import jax
import jax.numpy as jnp
from jax import lax
from jax.experimental import pallas as pl
from jax.experimental.pallas import tpu as pltpu
from jax.sharding import PartitionSpec as P

MESH = pl.DeviceIdType.MESH
F32 = jnp.float32
BF16 = jnp.bfloat16
BEST = lax.Precision.HIGHEST
LANES = 128


def dot_nt(a, b):
    return lax.dot_general(a, b, (((1,), (1,)), ((), ())), preferred_element_type=F32)


def dot_nn(a, b):
    return jnp.dot(a, b, preferred_element_type=F32)


def unit(rows, cols):
    down = lax.broadcasted_iota(jnp.int32, (rows, cols), 0)
    along = lax.broadcasted_iota(jnp.int32, (rows, cols), 1)
    return (down == along).astype(F32).astype(BF16)


def layer_kernel(
    n,
    q_ref,
    k_ref,
    v_ref,
    rate_ref,
    res_ref,
    proj_ref,
    routes_ref,
    shares_ref,
    gate_hbm,
    up_hbm,
    down_hbm,
    out_ref,
    states,
    attns,
    give,
    mine,
    got,
    passed,
    land,
    res_both,
    routes_both,
    shares_both,
    turned_stream,
    leaving,
    arrived,
    tokens,
    hidden,
    product,
    half_give,
    half_got,
    turned_out,
    back,
    home,
    last,
    w_gate,
    w_up,
    w_down,
    s_send,
    s_recv,
    a_send,
    a_recv,
    t_send,
    t_recv,
    h_send,
    h_recv,
    x_send,
    x_recv,
    pair_send,
    pair_recv,
    sum_send,
    sum_recv,
    go_send,
    go_recv,
    back_send,
    back_recv,
    few_send,
    few_recv,
    w_sem,
):
    me = lax.axis_index("ctx")
    col = lax.axis_index("exp")
    chip = col // 2
    core = lax.rem(col, 2)
    partner = col + 1 - 2 * core
    half = n // 2
    near = (lax.rem(me + 1, n), lax.rem(me + n - 1, n))
    count, wide = q_ref.shape
    heads = rate_ref.shape[0]
    width = wide // heads
    own_rows, slice_width = res_ref.shape
    part_width = slice_width // 2
    slots = hidden.shape[-1]
    capacity = leaving.shape[2]
    lanes_out = n * capacity

    def remote(src, dst, send_sem, recv_sem, **where):
        return pltpu.make_async_remote_copy(
            src_ref=src,
            dst_ref=dst,
            send_sem=send_sem,
            recv_sem=recv_sem,
            device_id=where,
            device_id_type=MESH,
        )

    weights = [
        pltpu.make_async_copy(src.at[0], dst, w_sem.at[i])
        for i, (src, dst) in enumerate(((gate_hbm, w_gate), (up_hbm, w_up), (down_hbm, w_down)))
    ]
    for copy in weights:
        copy.start()

    barrier = pltpu.get_barrier_semaphore()
    for peer in near:
        pl.semaphore_signal(barrier, inc=1, device_id={"ctx": peer}, device_id_type=MESH)
    pl.semaphore_signal(barrier, inc=1, device_id={"exp": partner}, device_id_type=MESH)

    def greet(j, carry):
        peer = 2 * lax.rem(chip + j, n) + core
        pl.semaphore_signal(barrier, inc=1, device_id={"exp": peer}, device_id_type=MESH)
        return carry

    lax.fori_loop(1, n, greet, 0)

    down_iota = lax.broadcasted_iota(jnp.int32, (count, width), 0).astype(F32)
    along_iota = lax.broadcasted_iota(jnp.int32, (count, width), 1).astype(F32)
    head_at = [slice(h * width, (h + 1) * width) for h in range(heads)]
    for h in range(heads):
        faded = k_ref[:, head_at[h]].astype(F32) * jnp.exp(-rate_ref[h] * (count - down_iota))
        local = jnp.dot(
            faded.T, v_ref[:, head_at[h]].astype(F32), precision=BEST, preferred_element_type=F32
        ).astype(BF16)
        states[me, 2 * h] = local[: width // 2]
        states[me, 2 * h + 1] = local[width // 2 :]
    res_both[pl.ds(pl.multiple_of(core * own_rows, own_rows), own_rows), :] = res_ref[...]
    routes_both[core] = routes_ref[...]
    shares_both[core] = shares_ref[...]
    pl.semaphore_wait(barrier, n + 2)

    rows_mine = res_both.at[pl.ds(pl.multiple_of(core * own_rows, own_rows), own_rows), :]
    rows_other = res_both.at[pl.ds(pl.multiple_of((1 - core) * own_rows, own_rows), own_rows), :]
    early = [
        (remote(res_ref, rows_mine, few_send.at[0], few_recv.at[0], exp=partner), rows_other),
        (
            remote(routes_ref, routes_both.at[core], few_send.at[1], few_recv.at[1], exp=partner),
            routes_both.at[1 - core],
        ),
        (
            remote(shares_ref, shares_both.at[core], few_send.at[2], few_recv.at[2], exp=partner),
            shares_both.at[1 - core],
        ),
    ]

    def origin_of(way, step):
        return lax.rem(me - step + n, n) if way == 0 else lax.rem(me + step, n)

    def ring(place, chunks, send, recv, work, forward=None):
        def hop(way, step, chunk):
            spot = place(origin_of(way, step), chunk)
            sems = (send.at[way, step, chunk], recv.at[way, step, chunk])
            return remote(spot, spot, *sems, ctx=near[way])

        def landed(way, step, chunk):
            spot = place(origin_of(way, step + 1), chunk)
            sems = (send.at[way, step, chunk], recv.at[way, step, chunk])
            return remote(spot, spot, *sems, ctx=near[way])

        def ends(way, chunk):
            return (chunk < chunks // 2) == (way == 0)

        every = [(chunk, way) for chunk in range(chunks) for way in range(2)]
        last_hop = [(chunk, way) for chunk, way in every if ends(way, chunk)]

        def turn(step, arriving, going):
            for chunk, way in every:
                if (chunk, way) in arriving:
                    landed(way, step - 1, chunk).wait_recv()
                if (chunk, way) in going:
                    hop(way, step, chunk).start()
                if forward is not None and (chunk, way) in arriving:
                    forward(way, step - 1, chunk).start()

        turn(0, [], every)
        work(0, [me])
        turn(1, every, every)
        work(1, [origin_of(0, 1), origin_of(1, 1)])

        def middle(step, carry):
            turn(step, every, every)
            work(step, [origin_of(0, step), origin_of(1, step)])
            return carry

        lax.fori_loop(2, half - 1, middle, 0)
        turn(half - 1, every, last_hop)
        work(half - 1, [origin_of(0, half - 1), origin_of(1, half - 1)])
        turn(half, last_hop, [])
        work(half, [origin_of(0, half)])

        def drain():
            def sent(step, carry):
                for chunk, way in every:
                    hop(way, step, chunk).wait_send()
                return carry

            lax.fori_loop(0, half - 1, sent, 0)
            for chunk, way in last_hop:
                hop(way, half - 1, chunk).wait_send()

        return drain

    lags = down_iota - along_iota
    inner = []

    def inside(step, origins):
        if isinstance(step, int) and step == 0:
            for copy, _ in early:
                copy.start()
            for h in range(heads):
                scores = dot_nt(q_ref[:, head_at[h]], k_ref[:, head_at[h]])
                keep = jnp.where(lags >= 0, jnp.exp(-rate_ref[h] * jnp.maximum(lags, 0.0)), 0.0)
                inner.append(dot_nn((scores * keep).astype(BF16), v_ref[:, head_at[h]]))

    drains = [ring(lambda o, c: states.at[o, c], states.shape[1], s_send, s_recv, inside)]
    for h in range(heads):

        def add_state(j, total, h=h):
            between = me - 1 - j
            span = jnp.full((1, width), jnp.maximum(between, 0)).astype(F32)
            fade = jnp.where(between >= 0, jnp.exp(-rate_ref[h] * count * span), 0.0)
            return total + fade * states[j, pl.ds(2 * h, 2)].reshape(width, width).astype(F32)

        earlier = lax.fori_loop(0, n, add_state, jnp.zeros((width, width), F32))
        across = jnp.dot(
            q_ref[:, head_at[h]].astype(F32), earlier, precision=BEST, preferred_element_type=F32
        )
        mixed = inner[h] + across * jnp.exp(-rate_ref[h] * down_iota)
        scale = lax.rsqrt(jnp.mean(mixed * mixed, axis=-1, keepdims=True) + 1e-06)
        attn = (mixed * scale).astype(BF16)
        piece = count // attns.shape[1]
        for c in range(attns.shape[1]):
            attns[me, c, :, head_at[h]] = attn[c * piece : (c + 1) * piece]

    def pair_copy(o):
        return remote(give.at[o], got.at[o], pair_send.at[o], pair_recv.at[o], exp=partner)

    def sum_copy(o):
        sems = (sum_send.at[o], sum_recv.at[chip])
        return remote(passed.at[o], land.at[chip], *sems, exp=2 * o + core)

    def split(value):
        low, high = value[:part_width], value[part_width:]
        return jnp.where(core == 0, low, high), jnp.where(core == 0, high, low)

    def project(o):
        block = attns[o].reshape(count, wide)
        kept, given = split(dot_nt(proj_ref[...], block))
        mine[o] = kept
        give[o] = given.astype(BF16)
        pair_copy(o).start()

    def hand_on(o):
        pair_copy(o).wait_recv()
        total = (mine[o] + got[o].astype(F32)).astype(BF16)

        @pl.when(o == chip)
        def _():
            land[o] = total

        @pl.when(o != chip)
        def _():
            passed[o] = total
            sum_copy(o).start()

    def out_step(step, origins):
        for o in origins:
            project(o)
        if isinstance(step, int) and step == 1:
            hand_on(me)
        elif not (isinstance(step, int) and step == 0):
            hand_on(origin_of(0, step - 1))
            hand_on(origin_of(1, step - 1))
        if isinstance(step, int) and step == half:
            hand_on(origin_of(0, half))

    drains.append(ring(lambda o, c: attns.at[o, c], attns.shape[1], a_send, a_recv, out_step))

    for copy, spot in early:
        copy.wait_send()
    for i, (copy, spot) in enumerate(early):
        remote(spot, spot, few_send.at[i], few_recv.at[i], exp=partner).wait_recv()

    lane = lax.broadcasted_iota(jnp.int32, (own_rows, lanes_out), 1)
    expert_of, slot_of = lane // capacity, lax.rem(lane, capacity)
    before = (
        lax.broadcasted_iota(jnp.int32, (own_rows, own_rows), 0)
        > lax.broadcasted_iota(jnp.int32, (own_rows, own_rows), 1)
    ).astype(F32)
    flip = unit(lanes_out, lanes_out)
    pickers, combiners = [], []
    for b in range(2):
        first = (routes_both[b, :, 0:1] == expert_of).astype(F32)
        second = (routes_both[b, :, 1:2] == expert_of).astype(F32)
        named = first + second
        rank = dot_nn(before.astype(BF16), named.astype(BF16))
        placed = jnp.where(rank == slot_of.astype(F32), named, 0.0)
        part = shares_both[b].astype(F32)
        whole = part[:, 0:1] + part[:, 1:2]
        combiners.append(placed * (first * (part[:, 0:1] / whole) + second * (part[:, 1:2] / whole)))
        pickers.append(dot_nt(flip, placed.astype(BF16)).astype(BF16))

    choose = (
        lax.broadcasted_iota(jnp.int32, (part_width, slice_width), 0) + core * part_width
        == lax.broadcasted_iota(jnp.int32, (part_width, slice_width), 1)
    ).astype(F32)
    start = dot_nt(choose.astype(BF16), res_both[...])

    def sum_landed(p):
        sems = (sum_send.at[p], sum_recv.at[p])
        return remote(land.at[p], land.at[p], *sems, exp=2 * p + core)

    def add_part(j, total):
        p = lax.rem(chip + j, n)

        @pl.when(j > 0)
        def _():
            sum_landed(p).wait_recv()

        return total + land[p].astype(F32)

    stream = lax.fori_loop(0, n, add_part, jnp.zeros((part_width, count), F32))
    stream = (stream + start).astype(BF16)
    turned_stream[pl.ds(part_width, LANES - part_width), :] = jnp.zeros(
        (LANES - part_width, count), BF16
    )
    turned_stream[pl.ds(0, part_width), :] = stream
    by_token = dot_nt(unit(count, count), turned_stream[...]).astype(BF16)
    by_block = [by_token[:own_rows], by_token[own_rows:]]

    def exchange(src, dst, send, recv):
        def outward(j):
            p = lax.rem(chip + j, n)
            return remote(src.at[p], dst.at[chip], send.at[p], recv.at[chip], exp=2 * p + core)

        def inward(j):
            p = lax.rem(chip + j, n)
            return remote(dst.at[p], dst.at[p], send.at[p], recv.at[p], exp=2 * p + core)

        def launch(j, carry):
            outward(j).start()
            return carry

        def finish(j, carry):
            inward(j).wait_recv()
            return carry

        def sent(j, carry):
            outward(j).wait_send()
            return carry

        lax.fori_loop(1, n, launch, 0)
        dst[chip] = src[chip]
        lax.fori_loop(1, n, finish, 0)
        drains.append(lambda: lax.fori_loop(1, n, sent, 0))

    for b in range(2):
        picked = dot_nn(pickers[b], by_block[b]).astype(BF16)
        leaving[:, b] = picked.reshape(n, capacity, LANES)
    exchange(leaving, arrived, go_send, go_recv)

    turned = dot_nt(unit(part_width, LANES), arrived[...].reshape(slots, LANES)).astype(BF16)
    chunks = tokens.shape[2]
    piece = part_width // chunks
    for c in range(chunks):
        tokens[me, core, c] = turned[c * piece : (c + 1) * piece]

    def hand_across(way, step, chunk):
        spot = tokens.at[origin_of(way, step + 1), core, chunk]
        sems = (x_send.at[way, step, chunk], x_recv.at[way, step, chunk])
        return remote(spot, spot, *sems, exp=partner)

    def handed(way, step, chunk):
        spot = tokens.at[origin_of(way, step + 1), 1 - core, chunk]
        sems = (x_send.at[way, step, chunk], x_recv.at[way, step, chunk])
        return remote(spot, spot, *sems, exp=partner)

    def own_across(side):
        spot = tokens.at[me, side]
        return remote(spot, spot, few_send.at[3], few_recv.at[3], exp=partner)

    def start_own(step, origins):
        if isinstance(step, int) and step == 0:
            own_across(core).start()

    drains.append(
        ring(lambda o, c: tokens.at[o, core, c], chunks, t_send, t_recv, start_own, hand_across)
    )
    own_across(1 - core).wait_recv()
    ways = [(chunk, way) for chunk in range(chunks) for way in range(2)]

    def all_handed(step, carry):
        for chunk, way in ways:
            handed(way, step, chunk).wait_recv()
        return carry

    lax.fori_loop(0, half - 1, all_handed, 0)
    ending = [(chunk, way) for chunk, way in ways if (chunk < chunks // 2) == (way == 0)]
    for chunk, way in ending:
        handed(way, half - 1, chunk).wait_recv()

    def across_sent():
        def sent(step, carry):
            for chunk, way in ways:
                hand_across(way, step, chunk).wait_send()
            return carry

        lax.fori_loop(0, half - 1, sent, 0)
        for chunk, way in ending:
            hand_across(way, half - 1, chunk).wait_send()
        own_across(core).wait_send()

    drains.append(across_sent)

    for copy in weights:
        copy.wait()
    group = 4
    gate = upper = square = 0.0
    for i in range(n // group):
        block = tokens[pl.ds(i * group, group)].reshape(group * slice_width, slots)
        span = slice(i * group * slice_width, (i + 1) * group * slice_width)
        gate += dot_nn(w_gate[:, span], block)
        upper += dot_nn(w_up[:, span], block)
        wide_block = block.astype(F32)
        square += jnp.sum(wide_block * wide_block, axis=0, keepdims=True)
    scale = lax.rsqrt(square / (n * slice_width) + 1e-06)
    gate = gate * scale
    unit_rows = (gate / (1.0 + jnp.exp(-gate)) * (upper * scale)).astype(BF16)
    units = unit_rows.shape[0]
    piece = units // hidden.shape[1]
    for c in range(hidden.shape[1]):
        hidden[me, c] = unit_rows[c * piece : (c + 1) * piece]

    def down_step(step, origins):
        for o in origins:
            at = pl.ds(pl.multiple_of(o * units, units), units)
            term = dot_nn(w_down[:, at], hidden[o].reshape(units, slots))
            if isinstance(step, int) and step == 0:
                product[...] = term
            else:
                product[...] += term

    drains.append(ring(lambda o, c: hidden.at[o, c], hidden.shape[1], h_send, h_recv, down_step))

    kept, given = split(product[...])
    half_give[...] = given.astype(BF16)
    swap = remote(half_give, half_got, few_send.at[4], few_recv.at[4], exp=partner)
    swap.start()
    swap.wait_recv()
    turned_out[pl.ds(part_width, LANES - part_width), :] = jnp.zeros(
        (LANES - part_width, slots), BF16
    )
    turned_out[pl.ds(0, part_width), :] = (kept + half_got[...].astype(F32)).astype(BF16)
    owners = LANES // (2 * capacity)
    for j in range(slots // LANES):
        rows = dot_nt(unit(LANES, LANES), turned_out[:, j * LANES : (j + 1) * LANES])
        back[pl.ds(j * owners, owners)] = rows.astype(BF16).reshape(owners, 2, capacity, LANES)
    exchange(back, home, back_send, back_recv)

    final = []
    for b in range(2):
        outs = home[:, b].reshape(lanes_out, LANES).astype(F32)
        mixed = jnp.dot(combiners[b], outs, precision=BEST, preferred_element_type=F32)
        final.append(by_block[b].astype(F32) + mixed)
    last[...] = jnp.where(core == 0, final[1], final[0]).astype(BF16)
    swap_last = remote(last, out_ref.at[core], few_send.at[5], few_recv.at[5], exp=partner)
    swap_last.start()
    out_ref[core] = jnp.where(core == 0, final[0], final[1]).astype(BF16)

    for drain in drains:
        drain()

    def pairs_sent(o, carry):
        pair_copy(o).wait_send()
        return carry

    lax.fori_loop(0, n, pairs_sent, 0)

    def sums_sent(j, carry):
        sum_copy(lax.rem(chip + j, n)).wait_send()
        return carry

    lax.fori_loop(1, n, sums_sent, 0)
    swap.wait_send()
    swap_last.wait_send()
    spot = out_ref.at[1 - core]
    remote(spot, spot, few_send.at[5], few_recv.at[5], exp=partner).wait_recv()


def body(
    queries,
    key_rows,
    value_rows,
    decay_rate,
    residual,
    out_proj,
    routes,
    gate_shares,
    gate_proj,
    up_proj,
    down_proj,
):
    n = lax.axis_size("ctx")
    holders = lax.axis_size("exp")
    count, wide = queries.shape
    heads = decay_rate.shape[0]
    width = wide // heads
    own_rows, slice_width = residual.shape
    part_width = slice_width // 2
    capacity = 2 * own_rows * routes.shape[1] // n
    slots = holders * capacity
    units = gate_proj.shape[1]
    vmem, dma = pltpu.VMEM, pltpu.SemaphoreType.DMA
    on_chip = pl.BlockSpec(memory_space=pltpu.VMEM)
    anywhere = pl.BlockSpec(memory_space=pl.ANY)
    half = n // 2
    ring4, ring2, each = dma((2, half, 4)), dma((2, half, 2)), dma((n,))
    out = pl.pallas_call(
        functools.partial(layer_kernel, n),
        out_shape=jax.ShapeDtypeStruct((2, own_rows, LANES), BF16),
        in_specs=[on_chip] * 3
        + [pl.BlockSpec(memory_space=pltpu.SMEM)]
        + [on_chip] * 4
        + [anywhere] * 3,
        out_specs=on_chip,
        scratch_shapes=[
            vmem((n, 2 * heads, width // 2, width), BF16),
            vmem((n, 4, count // 4, wide), BF16),
            vmem((n, part_width, count), BF16),
            vmem((n, part_width, count), F32),
            vmem((n, part_width, count), BF16),
            vmem((n, part_width, count), BF16),
            vmem((n, part_width, count), BF16),
            vmem((2 * own_rows, slice_width), BF16),
            vmem((2,) + routes.shape, jnp.int32),
            vmem((2,) + routes.shape, jnp.int32),
            vmem((LANES, count), BF16),
            vmem((n, 2, capacity, LANES), BF16),
            vmem((n, 2, capacity, LANES), BF16),
            vmem((n, 2, 2, part_width // 2, slots), BF16),
            vmem((n, 4, units // 4, slots), BF16),
            vmem((slice_width, slots), F32),
            vmem((part_width, slots), BF16),
            vmem((part_width, slots), BF16),
            vmem((LANES, slots), BF16),
            vmem((n, 2, capacity, LANES), BF16),
            vmem((n, 2, capacity, LANES), BF16),
            vmem((own_rows, LANES), BF16),
            vmem(gate_proj.shape[1:], BF16),
            vmem(up_proj.shape[1:], BF16),
            vmem(down_proj.shape[1:], BF16),
        ]
        + [ring4] * 4
        + [ring2] * 2
        + [ring4] * 2
        + [ring2] * 2
        + [each] * 8
        + [dma((6,))] * 2
        + [dma((3,))],
        compiler_params=pltpu.CompilerParams(
            collective_id=0, has_side_effects=True, vmem_limit_bytes=56 * 2**20
        ),
        name="layer",
    )(
        queries,
        key_rows,
        value_rows,
        decay_rate,
        residual,
        out_proj.T,
        routes,
        gate_shares,
        gate_proj,
        up_proj,
        down_proj,
    )
    return jnp.concatenate([out[0, :, :part_width], out[1, :, :part_width]], axis=1)


def solution(mesh):
    in_specs = (
        P("ctx", "exp"),
        P("ctx", "exp"),
        P("ctx", "exp"),
        P("exp"),
        P("exp", "ctx"),
        P("exp", "ctx"),
        P("exp", None),
        P("exp", None),
        P("exp", "ctx", None),
        P("exp", "ctx", None),
        P("exp", "ctx", None),
    )
    out_specs = P("exp", "ctx")
    return jax.shard_map(body, mesh=mesh, in_specs=in_specs, out_specs=out_specs, check_vma=False)
```

time: 477 us -> 181 us (0.38)
  waiting for transfers between devices: 296 us -> 0 us
  Pallas kernels: 0 us -> 177 us
  blocking collectives: 111 us -> 0 us
  starting transfers between devices: 18.2 us -> 0 us
  other arithmetic: 18.3 us -> 0.7 us
  between operations: 14 us -> 0.01 us
  matrix products: 13.4 us -> 0 us
    all_gather x3 -> x0, waiting for transfers between devices: 181 us -> none  [the longest x1 79.8 us: body(): lax.all_gather(hidden, 'ctx', axis=1, tiled=True)]
    pallas_call x0 -> x1, Pallas kernels: none -> 177 us  [body(): pl.pallas_call(functools.partial(layer_kernel, n), out_shape=jax.ShapeDty...]
    reduce_scatter x1 -> x0, waiting for transfers between devices: 107 us -> none  [body(): lax.psum_scatter(jnp.dot(all_heads, out_proj, preferred_element_type=jnp....]
    all_to_all x1 -> x0, blocking collectives: 52.9 us -> none  [body(): lax.all_to_all(jnp.broadcast_to(shaped, (experts, 2, capacity, feats)).re...]
    unnamed x1 -> x0, blocking collectives: 31.5 us -> none
    all_gather x1 -> x0, blocking collectives: 26.8 us -> none  [body(): whole = lax.all_gather(stream, 'ctx', axis=1, tiled=True)]
    all_to_all x1 -> x0, starting transfers between devices: 18 us -> none  [body(): lax.all_to_all(leaving.astype(jnp.bfloat16), 'exp', split_axis=0, concat_...]
    select_n x16 -> x0, other arithmetic: 14.9 us -> none  [step(): return jax.tree.map(lambda a, b: jnp.where(reached, a, b), new, before)]
  transfers between devices with their start and end apart: 5 -> 0, of which waited for: 5 -> 0; matrix products, arithmetic and copies ran while one was open for 1% -> 0% of each run, Pallas kernels for 0% -> 0%
where the time goes in v2:
time: 181 us
  Pallas kernels  177 us (98%)
  local copies, waits for them, and re-layouts  3.5 us (2%)
    pallas_call x1, Pallas kernels, body(): pl.pallas_call(functools.partial(layer_kernel, n), out_shape=jax.ShapeDty...  177 us

profile of v2, /device:TPU:1, one launch (start us, length us, event | category | flops | bytes accessed | tf_op | source)
XLA Modules:
  0.0 181.1 jit_solution(15468659487126995760)
XLA Ops:
  0.0 1.4 copy.12.routes_ref
  1.4 1.4 copy.13.shares_ref
  2.8 176.9 %layer.1 = bf16[2,64,128]{2,1,0:T(8,128)(2,1)} custom-call(bf16[128,256]{1,0:T(8,128)(2,1)} %q_ref.1, bf16[128,256]{1,0:T(8,128)(2,1)} %k_ref.1, bf16[128,256]{1,0:T(8,128)(2,1)} %v_ref.1, f32[2]{0:T(128)} %rate_ref.1, bf16[64,192]{1,0:T(8,128)(2,1)} %res_ref.1, bf16[192,256]{1,0:T(8,128)(2,1)} %bitcast.5, s32[64,2]{1,0:T(8,128)} %copy.12.routes_ref, ...), custom_call_target="tpu_custom_call" | custom-call | tf_op jit(solution)/shard_map/layer/pallas_call | solution.py:537
  179.7 0.7 slice_bitcast_fusion.1
  180.4 0.7 pad_maximum_fusion

commit v3 on v2

--- a/solution.py
+++ b/solution.py
@@ -66,6 +66,9 @@
     w_gate,
     w_up,
     w_down,
+    gate_sum,
+    up_sum,
+    square,
     s_send,
     s_recv,
     a_send,
@@ -94,7 +97,10 @@
     core = lax.rem(col, 2)
     partner = col + 1 - 2 * core
     half = n // 2
-    near = (lax.rem(me + 1, n), lax.rem(me + n - 1, n))
+
+    def along(way, steps):
+        return lax.rem(me + steps, n) if way == 0 else lax.rem(me - steps + n, n)
+
     count, wide = q_ref.shape
     heads = rate_ref.shape[0]
     width = wide // heads
@@ -122,8 +128,10 @@
         copy.start()
 
     barrier = pltpu.get_barrier_semaphore()
-    for peer in near:
-        pl.semaphore_signal(barrier, inc=1, device_id={"ctx": peer}, device_id_type=MESH)
+    for steps in (1, 2):
+        for way in range(2):
+            peer = along(way, steps)
+            pl.semaphore_signal(barrier, inc=1, device_id={"ctx": peer}, device_id_type=MESH)
     pl.semaphore_signal(barrier, inc=1, device_id={"exp": partner}, device_id_type=MESH)
 
     def greet(j, carry):
@@ -134,7 +142,7 @@
     lax.fori_loop(1, n, greet, 0)
 
     down_iota = lax.broadcasted_iota(jnp.int32, (count, width), 0).astype(F32)
-    along_iota = lax.broadcasted_iota(jnp.int32, (count, width), 1).astype(F32)
+    right_iota = lax.broadcasted_iota(jnp.int32, (count, width), 1).astype(F32)
     head_at = [slice(h * width, (h + 1) * width) for h in range(heads)]
     for h in range(heads):
         faded = k_ref[:, head_at[h]].astype(F32) * jnp.exp(-rate_ref[h] * (count - down_iota))
@@ -146,7 +154,7 @@
     res_both[pl.ds(pl.multiple_of(core * own_rows, own_rows), own_rows), :] = res_ref[...]
     routes_both[core] = routes_ref[...]
     shares_both[core] = shares_ref[...]
-    pl.semaphore_wait(barrier, n + 2)
+    pl.semaphore_wait(barrier, n + 4)
 
     rows_mine = res_both.at[pl.ds(pl.multiple_of(core * own_rows, own_rows), own_rows), :]
     rows_other = res_both.at[pl.ds(pl.multiple_of((1 - core) * own_rows, own_rows), own_rows), :]
@@ -163,63 +171,69 @@
     ]
 
     def origin_of(way, step):
-        return lax.rem(me - step + n, n) if way == 0 else lax.rem(me + step, n)
-
-    def ring(place, chunks, send, recv, work, forward=None):
-        def hop(way, step, chunk):
+        return along(1 - way, step)
+
+    def ring(place, chunks, send, recv, work, forward=None, skip=False):
+        def hop(way, step, stride, chunk):
+            spot = place(origin_of(way, step - stride), chunk)
+            sems = (send.at[way, step - 1, chunk], recv.at[way, step - 1, chunk])
+            return remote(spot, spot, *sems, ctx=along(way, stride))
+
+        def landed(way, step, chunk):
             spot = place(origin_of(way, step), chunk)
-            sems = (send.at[way, step, chunk], recv.at[way, step, chunk])
-            return remote(spot, spot, *sems, ctx=near[way])
-
-        def landed(way, step, chunk):
-            spot = place(origin_of(way, step + 1), chunk)
-            sems = (send.at[way, step, chunk], recv.at[way, step, chunk])
-            return remote(spot, spot, *sems, ctx=near[way])
-
-        def ends(way, chunk):
-            return (chunk < chunks // 2) == (way == 0)
+            sems = (send.at[way, step - 1, chunk], recv.at[way, step - 1, chunk])
+            return remote(spot, spot, *sems, ctx=along(way, 1))
 
         every = [(chunk, way) for chunk in range(chunks) for way in range(2)]
-        last_hop = [(chunk, way) for chunk, way in every if ends(way, chunk)]
-
-        def turn(step, arriving, going):
+        last_hop = [(chunk, way) for chunk, way in every if (chunk < chunks // 2) == (way == 0)]
+
+        def turn(step, even, arriving, far, close):
             for chunk, way in every:
                 if (chunk, way) in arriving:
-                    landed(way, step - 1, chunk).wait_recv()
-                if (chunk, way) in going:
-                    hop(way, step, chunk).start()
+                    landed(way, step, chunk).wait_recv()
+                if skip and even and (chunk, way) in far:
+                    hop(way, step + 2, 2, chunk).start()
+                if (not skip or even) and (chunk, way) in close:
+                    hop(way, step + 1, 1, chunk).start()
                 if forward is not None and (chunk, way) in arriving:
-                    forward(way, step - 1, chunk).start()
-
-        turn(0, [], every)
+                    forward(way, step, chunk).start()
+
+        def both(step):
+            return [origin_of(0, step), origin_of(1, step)]
+
+        turn(0, True, [], every, every)
         work(0, [me])
-        turn(1, every, every)
-        work(1, [origin_of(0, 1), origin_of(1, 1)])
-
-        def middle(step, carry):
-            turn(step, every, every)
-            work(step, [origin_of(0, step), origin_of(1, step)])
+        turn(1, False, every, every, every)
+        work(1, both(1))
+
+        def middle(i, carry):
+            turn(2 * i, True, every, every, every)
+            work(2 * i, both(2 * i))
+            turn(2 * i + 1, False, every, every, every)
+            work(2 * i + 1, both(2 * i + 1))
             return carry
 
-        lax.fori_loop(2, half - 1, middle, 0)
-        turn(half - 1, every, last_hop)
-        work(half - 1, [origin_of(0, half - 1), origin_of(1, half - 1)])
-        turn(half, last_hop, [])
+        lax.fori_loop(1, half // 2 - 1, middle, 0)
+        turn(half - 2, True, every, last_hop, every)
+        work(half - 2, both(half - 2))
+        turn(half - 1, False, every, [], last_hop)
+        work(half - 1, both(half - 1))
+        turn(half, True, last_hop, [], [])
         work(half, [origin_of(0, half)])
 
         def drain():
             def sent(step, carry):
                 for chunk, way in every:
-                    hop(way, step, chunk).wait_send()
+                    landed(way, step, chunk).wait_send()
                 return carry
 
-            lax.fori_loop(0, half - 1, sent, 0)
+            lax.fori_loop(1, half, sent, 0)
             for chunk, way in last_hop:
-                hop(way, half - 1, chunk).wait_send()
+                landed(way, half, chunk).wait_send()
 
         return drain
 
-    lags = down_iota - along_iota
+    lags = down_iota - right_iota
     inner = []
 
     def inside(step, origins):
@@ -231,7 +245,9 @@
                 keep = jnp.where(lags >= 0, jnp.exp(-rate_ref[h] * jnp.maximum(lags, 0.0)), 0.0)
                 inner.append(dot_nn((scores * keep).astype(BF16), v_ref[:, head_at[h]]))
 
-    drains = [ring(lambda o, c: states.at[o, c], states.shape[1], s_send, s_recv, inside)]
+    drains = [
+        ring(lambda o, c: states.at[o, c], states.shape[1], s_send, s_recv, inside, skip=True)
+    ]
     for h in range(heads):
 
         def add_state(j, total, h=h):
@@ -293,7 +309,9 @@
         if isinstance(step, int) and step == half:
             hand_on(origin_of(0, half))
 
-    drains.append(ring(lambda o, c: attns.at[o, c], attns.shape[1], a_send, a_recv, out_step))
+    drains.append(
+        ring(lambda o, c: attns.at[o, c], attns.shape[1], a_send, a_recv, out_step, skip=True)
+    )
 
     for copy, spot in early:
         copy.wait_send()
@@ -301,7 +319,8 @@
         remote(spot, spot, few_send.at[i], few_recv.at[i], exp=partner).wait_recv()
 
     lane = lax.broadcasted_iota(jnp.int32, (own_rows, lanes_out), 1)
-    expert_of, slot_of = lane // capacity, lax.rem(lane, capacity)
+    expert_of, slot_of = (lane // capacity).astype(F32), lax.rem(lane, capacity).astype(F32)
+    upright = unit(own_rows, own_rows)
     before = (
         lax.broadcasted_iota(jnp.int32, (own_rows, own_rows), 0)
         > lax.broadcasted_iota(jnp.int32, (own_rows, own_rows), 1)
@@ -309,12 +328,13 @@
     flip = unit(lanes_out, lanes_out)
     pickers, combiners = [], []
     for b in range(2):
-        first = (routes_both[b, :, 0:1] == expert_of).astype(F32)
-        second = (routes_both[b, :, 1:2] == expert_of).astype(F32)
+        chosen = dot_nt(upright, routes_both[b].astype(F32).astype(BF16))
+        first = (chosen[:, 0:1] == expert_of).astype(F32)
+        second = (chosen[:, 1:2] == expert_of).astype(F32)
         named = first + second
         rank = dot_nn(before.astype(BF16), named.astype(BF16))
-        placed = jnp.where(rank == slot_of.astype(F32), named, 0.0)
-        part = shares_both[b].astype(F32)
+        placed = jnp.where(rank == slot_of, named, 0.0)
+        part = dot_nt(upright, shares_both[b].astype(F32).astype(BF16))
         whole = part[:, 0:1] + part[:, 1:2]
         combiners.append(placed * (first * (part[:, 0:1] / whole) + second * (part[:, 1:2] / whole)))
         pickers.append(dot_nt(flip, placed.astype(BF16)).astype(BF16))
@@ -385,38 +405,51 @@
         tokens[me, core, c] = turned[c * piece : (c + 1) * piece]
 
     def hand_across(way, step, chunk):
-        spot = tokens.at[origin_of(way, step + 1), core, chunk]
-        sems = (x_send.at[way, step, chunk], x_recv.at[way, step, chunk])
+        spot = tokens.at[origin_of(way, step), core, chunk]
+        sems = (x_send.at[way, step - 1, chunk], x_recv.at[way, step - 1, chunk])
         return remote(spot, spot, *sems, exp=partner)
 
     def handed(way, step, chunk):
-        spot = tokens.at[origin_of(way, step + 1), 1 - core, chunk]
-        sems = (x_send.at[way, step, chunk], x_recv.at[way, step, chunk])
+        spot = tokens.at[origin_of(way, step), 1 - core, chunk]
+        sems = (x_send.at[way, step - 1, chunk], x_recv.at[way, step - 1, chunk])
         return remote(spot, spot, *sems, exp=partner)
 
     def own_across(side):
         spot = tokens.at[me, side]
         return remote(spot, spot, few_send.at[3], few_recv.at[3], exp=partner)
 
-    def start_own(step, origins):
+    ways = [(chunk, way) for chunk in range(chunks) for way in range(2)]
+    ending = [(chunk, way) for chunk, way in ways if (chunk < chunks // 2) == (way == 0)]
+
+    def multiply(step, arrivals):
+        for chunk, way in arrivals:
+            handed(way, step, chunk).wait_recv()
+        odd = lax.rem(me + step, 2) == 1
+        base = lax.rem(jnp.where(odd, me + step - 1, me - step + n), n)
+        block = tokens[pl.ds(base, 2)].reshape(2 * slice_width, slots)
+        span = pl.ds(pl.multiple_of(base * slice_width, 2 * slice_width), 2 * slice_width)
+        gate_sum[...] += dot_nn(w_gate[:, span], block)
+        up_sum[...] += dot_nn(w_up[:, span], block)
+        wide_block = block.astype(F32)
+        square[...] += jnp.sum(wide_block * wide_block, axis=0, keepdims=True)
+
+    def token_step(step, origins):
         if isinstance(step, int) and step == 0:
             own_across(core).start()
+            gate_sum[...] = jnp.zeros_like(gate_sum)
+            up_sum[...] = jnp.zeros_like(up_sum)
+            square[...] = jnp.zeros_like(square)
+        elif isinstance(step, int) and step == 1:
+            for copy in weights:
+                copy.wait()
+            own_across(1 - core).wait_recv()
+        else:
+            multiply(step - 1, ways)
 
     drains.append(
-        ring(lambda o, c: tokens.at[o, core, c], chunks, t_send, t_recv, start_own, hand_across)
+        ring(lambda o, c: tokens.at[o, core, c], chunks, t_send, t_recv, token_step, hand_across)
     )
-    own_across(1 - core).wait_recv()
-    ways = [(chunk, way) for chunk in range(chunks) for way in range(2)]
-
-    def all_handed(step, carry):
-        for chunk, way in ways:
-            handed(way, step, chunk).wait_recv()
-        return carry
-
-    lax.fori_loop(0, half - 1, all_handed, 0)
-    ending = [(chunk, way) for chunk, way in ways if (chunk < chunks // 2) == (way == 0)]
-    for chunk, way in ending:
-        handed(way, half - 1, chunk).wait_recv()
+    multiply(half, ending)
 
     def across_sent():
         def sent(step, carry):
@@ -424,27 +457,17 @@
                 hand_across(way, step, chunk).wait_send()
             return carry
 
-        lax.fori_loop(0, half - 1, sent, 0)
+        lax.fori_loop(1, half, sent, 0)
         for chunk, way in ending:
-            hand_across(way, half - 1, chunk).wait_send()
+            hand_across(way, half, chunk).wait_send()
         own_across(core).wait_send()
 
     drains.append(across_sent)
 
-    for copy in weights:
-        copy.wait()
-    group = 4
-    gate = upper = square = 0.0
-    for i in range(n // group):
-        block = tokens[pl.ds(i * group, group)].reshape(group * slice_width, slots)
-        span = slice(i * group * slice_width, (i + 1) * group * slice_width)
-        gate += dot_nn(w_gate[:, span], block)
-        upper += dot_nn(w_up[:, span], block)
-        wide_block = block.astype(F32)
-        square += jnp.sum(wide_block * wide_block, axis=0, keepdims=True)
-    scale = lax.rsqrt(square / (n * slice_width) + 1e-06)
-    gate = gate * scale
-    unit_rows = (gate / (1.0 + jnp.exp(-gate)) * (upper * scale)).astype(BF16)
+    scale = lax.rsqrt(square[...] / (n * slice_width) + 1e-06)
+    gate = gate_sum[...] * scale
+    upper = up_sum[...] * scale
+    unit_rows = (gate / (1.0 + jnp.exp(-gate)) * upper).astype(BF16)
     units = unit_rows.shape[0]
     piece = units // hidden.shape[1]
     for c in range(hidden.shape[1]):
@@ -533,7 +556,7 @@
     on_chip = pl.BlockSpec(memory_space=pltpu.VMEM)
     anywhere = pl.BlockSpec(memory_space=pl.ANY)
     half = n // 2
-    ring4, ring2, each = dma((2, half, 4)), dma((2, half, 2)), dma((n,))
+    ring4, ring3, each = dma((2, half, 4)), dma((2, half, 3)), dma((n,))
     out = pl.pallas_call(
         functools.partial(layer_kernel, n),
         out_shape=jax.ShapeDtypeStruct((2, own_rows, LANES), BF16),
@@ -551,12 +574,12 @@
             vmem((n, part_width, count), BF16),
             vmem((n, part_width, count), BF16),
             vmem((2 * own_rows, slice_width), BF16),
-            vmem((2,) + routes.shape, jnp.int32),
-            vmem((2,) + routes.shape, jnp.int32),
+            vmem((2,) + routes.shape[::-1], jnp.int32),
+            vmem((2,) + routes.shape[::-1], jnp.int32),
             vmem((LANES, count), BF16),
             vmem((n, 2, capacity, LANES), BF16),
             vmem((n, 2, capacity, LANES), BF16),
-            vmem((n, 2, 2, part_width // 2, slots), BF16),
+            vmem((n, 2, 3, part_width // 3, slots), BF16),
             vmem((n, 4, units // 4, slots), BF16),
             vmem((slice_width, slots), F32),
             vmem((part_width, slots), BF16),
@@ -568,11 +591,14 @@
             vmem(gate_proj.shape[1:], BF16),
             vmem(up_proj.shape[1:], BF16),
             vmem(down_proj.shape[1:], BF16),
+            vmem((units, slots), F32),
+            vmem((units, slots), F32),
+            vmem((1, slots), F32),
         ]
         + [ring4] * 4
-        + [ring2] * 2
+        + [ring3] * 2
         + [ring4] * 2
-        + [ring2] * 2
+        + [ring3] * 2
         + [each] * 8
         + [dma((6,))] * 2
         + [dma((3,))],
@@ -587,8 +613,8 @@
         decay_rate,
         residual,
         out_proj.T,
-        routes,
-        gate_shares,
+        routes.T,
+        gate_shares.T,
         gate_proj,
         up_proj,
         down_proj,

time: 181 us -> 169 us (0.934)
  Pallas kernels: 177 us -> 168 us
  local copies, waits for them, and re-layouts: 3.5 us -> 0.74 us
    pallas_call x1, Pallas kernels: 177 us -> 168 us  [body(): pl.pallas_call(functools.partial(layer_kernel, n), out_shape=jax.ShapeDty...]
    unnamed x2 -> x0, local copies, waits for them, and re-layouts: 2.76 us -> none
where the time goes in v3:
time: 169 us
  Pallas kernels  168 us (99%)
    pallas_call x1, Pallas kernels, body(): pl.pallas_call(functools.partial(layer_kernel, n), out_shape=jax.ShapeDty...  168 us

profile of v3, /device:TPU:1, one launch (start us, length us, event | category | flops | bytes accessed | tf_op | source)
XLA Modules:
  0.0 169.1 jit_solution(10623485289611651689)
XLA Ops:
  0.0 167.7 %layer.1 = bf16[2,64,128]{2,1,0:T(8,128)(2,1)} custom-call(bf16[128,256]{1,0:T(8,128)(2,1)} %q_ref.1, bf16[128,256]{1,0:T(8,128)(2,1)} %k_ref.1, bf16[128,256]{1,0:T(8,128)(2,1)} %v_ref.1, f32[2]{0:T(128)} %rate_ref.1, bf16[64,192]{1,0:T(8,128)(2,1)} %res_ref.1, bf16[192,256]{1,0:T(8,128)(2,1)} %bitcast.7, s32[2,64]{1,0:T(2,128)} %bitcast.8, ...), custom_call_target="tpu_custom_call" | custom-call | tf_op jit(solution)/shard_map/layer/pallas_call | solution.py:560
  167.7 0.7 slice_bitcast_fusion.1
  168.4 0.7 pad_maximum_fusion

commit v4 on v3

--- a/solution.py
+++ b/solution.py
@@ -57,8 +57,8 @@
     tokens,
     hidden,
     product,
-    half_give,
-    half_got,
+    earlier,
+    streams,
     turned_out,
     back,
     home,
@@ -132,14 +132,15 @@
         for way in range(2):
             peer = along(way, steps)
             pl.semaphore_signal(barrier, inc=1, device_id={"ctx": peer}, device_id_type=MESH)
-    pl.semaphore_signal(barrier, inc=1, device_id={"exp": partner}, device_id_type=MESH)
+
+    holders = 2 * n
 
     def greet(j, carry):
-        peer = 2 * lax.rem(chip + j, n) + core
+        peer = lax.rem(col + j, holders)
         pl.semaphore_signal(barrier, inc=1, device_id={"exp": peer}, device_id_type=MESH)
         return carry
 
-    lax.fori_loop(1, n, greet, 0)
+    lax.fori_loop(1, holders, greet, 0)
 
     down_iota = lax.broadcasted_iota(jnp.int32, (count, width), 0).astype(F32)
     right_iota = lax.broadcasted_iota(jnp.int32, (count, width), 1).astype(F32)
@@ -154,7 +155,7 @@
     res_both[pl.ds(pl.multiple_of(core * own_rows, own_rows), own_rows), :] = res_ref[...]
     routes_both[core] = routes_ref[...]
     shares_both[core] = shares_ref[...]
-    pl.semaphore_wait(barrier, n + 4)
+    pl.semaphore_wait(barrier, holders + 3)
 
     rows_mine = res_both.at[pl.ds(pl.multiple_of(core * own_rows, own_rows), own_rows), :]
     rows_other = res_both.at[pl.ds(pl.multiple_of((1 - core) * own_rows, own_rows), own_rows), :]
@@ -244,22 +245,24 @@
                 scores = dot_nt(q_ref[:, head_at[h]], k_ref[:, head_at[h]])
                 keep = jnp.where(lags >= 0, jnp.exp(-rate_ref[h] * jnp.maximum(lags, 0.0)), 0.0)
                 inner.append(dot_nn((scores * keep).astype(BF16), v_ref[:, head_at[h]]))
+            earlier[...] = jnp.zeros_like(earlier)
+            return
+        for j in origins:
+            between = me - 1 - j
+            span = jnp.full((1, width), jnp.maximum(between, 0)).astype(F32)
+            for h in range(heads):
+                fade = jnp.where(between >= 0, jnp.exp(-rate_ref[h] * count * span), 0.0)
+                state = states[j, pl.ds(2 * h, 2)].reshape(width, width)
+                earlier[h] += fade * state.astype(F32)
 
     drains = [
         ring(lambda o, c: states.at[o, c], states.shape[1], s_send, s_recv, inside, skip=True)
     ]
     for h in range(heads):
-
-        def add_state(j, total, h=h):
-            between = me - 1 - j
-            span = jnp.full((1, width), jnp.maximum(between, 0)).astype(F32)
-            fade = jnp.where(between >= 0, jnp.exp(-rate_ref[h] * count * span), 0.0)
-            return total + fade * states[j, pl.ds(2 * h, 2)].reshape(width, width).astype(F32)
-
-        earlier = lax.fori_loop(0, n, add_state, jnp.zeros((width, width), F32))
-        across = jnp.dot(
-            q_ref[:, head_at[h]].astype(F32), earlier, precision=BEST, preferred_element_type=F32
-        )
+        high = earlier[h].astype(BF16)
+        low = (earlier[h] - high.astype(F32)).astype(BF16)
+        query = q_ref[:, head_at[h]]
+        across = dot_nn(query, high) + dot_nn(query, low)
         mixed = inner[h] + across * jnp.exp(-rate_ref[h] * down_iota)
         scale = lax.rsqrt(jnp.mean(mixed * mixed, axis=-1, keepdims=True) + 1e-06)
         attn = (mixed * scale).astype(BF16)
@@ -366,6 +369,11 @@
     turned_stream[pl.ds(0, part_width), :] = stream
     by_token = dot_nt(unit(count, count), turned_stream[...]).astype(BF16)
     by_block = [by_token[:own_rows], by_token[own_rows:]]
+    last[...] = jnp.where(core == 0, by_block[1].astype(F32), by_block[0].astype(F32)).astype(BF16)
+    streams[core] = jnp.where(
+        core == 0, by_block[0].astype(F32), by_block[1].astype(F32)
+    ).astype(BF16)
+    swap = remote(last, streams.at[core], few_send.at[4], few_recv.at[4], exp=partner)
 
     def exchange(src, dst, send, recv):
         def outward(j):
@@ -397,6 +405,7 @@
         picked = dot_nn(pickers[b], by_block[b]).astype(BF16)
         leaving[:, b] = picked.reshape(n, capacity, LANES)
     exchange(leaving, arrived, go_send, go_recv)
+    swap.start()
 
     turned = dot_nt(unit(part_width, LANES), arrived[...].reshape(slots, LANES)).astype(BF16)
     chunks = tokens.shape[2]
@@ -484,31 +493,54 @@
 
     drains.append(ring(lambda o, c: hidden.at[o, c], hidden.shape[1], h_send, h_recv, down_step))
 
-    kept, given = split(product[...])
-    half_give[...] = given.astype(BF16)
-    swap = remote(half_give, half_got, few_send.at[4], few_recv.at[4], exp=partner)
-    swap.start()
-    swap.wait_recv()
-    turned_out[pl.ds(part_width, LANES - part_width), :] = jnp.zeros(
-        (LANES - part_width, slots), BF16
-    )
-    turned_out[pl.ds(0, part_width), :] = (kept + half_got[...].astype(F32)).astype(BF16)
-    owners = LANES // (2 * capacity)
+    for f in range(2):
+        turned_out[f, pl.ds(part_width, LANES - part_width), :] = jnp.zeros(
+            (LANES - part_width, slots), BF16
+        )
+        turned_out[f, pl.ds(0, part_width), :] = product[
+            pl.ds(f * part_width, part_width), :
+        ].astype(BF16)
+    owners = LANES // capacity
     for j in range(slots // LANES):
-        rows = dot_nt(unit(LANES, LANES), turned_out[:, j * LANES : (j + 1) * LANES])
-        back[pl.ds(j * owners, owners)] = rows.astype(BF16).reshape(owners, 2, capacity, LANES)
-    exchange(back, home, back_send, back_recv)
-
-    final = []
-    for b in range(2):
-        outs = home[:, b].reshape(lanes_out, LANES).astype(F32)
-        mixed = jnp.dot(combiners[b], outs, precision=BEST, preferred_element_type=F32)
-        final.append(by_block[b].astype(F32) + mixed)
-    last[...] = jnp.where(core == 0, final[1], final[0]).astype(BF16)
-    swap_last = remote(last, out_ref.at[core], few_send.at[5], few_recv.at[5], exp=partner)
-    swap_last.start()
-    out_ref[core] = jnp.where(core == 0, final[0], final[1]).astype(BF16)
-
+        for f in range(2):
+            rows = dot_nt(unit(LANES, LANES), turned_out[f, :, j * LANES : (j + 1) * LANES])
+            back[pl.ds(j * owners, owners), f] = rows.astype(BF16).reshape(owners, capacity, LANES)
+
+    def homeward(j):
+        peer = lax.rem(col + j, holders)
+        sems = (back_send.at[peer], back_recv.at[col])
+        return remote(back.at[peer], home.at[col], *sems, exp=peer)
+
+    def come_home(j):
+        peer = lax.rem(col + j, holders)
+        sems = (back_send.at[peer], back_recv.at[peer])
+        return remote(home.at[peer], home.at[peer], *sems, exp=peer)
+
+    def launch_home(j, carry):
+        homeward(j).start()
+        return carry
+
+    def finish_home(j, carry):
+        come_home(j).wait_recv()
+        return carry
+
+    def home_sent(j, carry):
+        homeward(j).wait_send()
+        return carry
+
+    lax.fori_loop(1, holders, launch_home, 0)
+    home[col] = back[col]
+    spot = streams.at[1 - core]
+    remote(spot, spot, few_send.at[4], few_recv.at[4], exp=partner).wait_recv()
+    combiner = jnp.where(core == 0, combiners[0], combiners[1])
+    lax.fori_loop(1, holders, finish_home, 0)
+    for f in range(2):
+        outs = home[:, f].reshape(n, 2, capacity, LANES).astype(F32)
+        outs = (outs[:, 0] + outs[:, 1]).astype(BF16).astype(F32).reshape(lanes_out, LANES)
+        mixed = jnp.dot(combiner, outs, precision=BEST, preferred_element_type=F32)
+        out_ref[f] = (streams[f].astype(F32) + mixed).astype(BF16)
+
+    lax.fori_loop(1, holders, home_sent, 0)
     for drain in drains:
         drain()
 
@@ -524,9 +556,6 @@
 
     lax.fori_loop(1, n, sums_sent, 0)
     swap.wait_send()
-    swap_last.wait_send()
-    spot = out_ref.at[1 - core]
-    remote(spot, spot, few_send.at[5], few_recv.at[5], exp=partner).wait_recv()
 
 
 def body(
@@ -582,11 +611,11 @@
             vmem((n, 2, 3, part_width // 3, slots), BF16),
             vmem((n, 4, units // 4, slots), BF16),
             vmem((slice_width, slots), F32),
-            vmem((part_width, slots), BF16),
-            vmem((part_width, slots), BF16),
-            vmem((LANES, slots), BF16),
-            vmem((n, 2, capacity, LANES), BF16),
-            vmem((n, 2, capacity, LANES), BF16),
+            vmem((heads, width, width), F32),
+            vmem((2, own_rows, LANES), BF16),
+            vmem((2, LANES, slots), BF16),
+            vmem((holders, 2, capacity, LANES), BF16),
+            vmem((holders, 2, capacity, LANES), BF16),
             vmem((own_rows, LANES), BF16),
             vmem(gate_proj.shape[1:], BF16),
             vmem(up_proj.shape[1:], BF16),
@@ -599,8 +628,9 @@
         + [ring3] * 2
         + [ring4] * 2
         + [ring3] * 2
-        + [each] * 8
-        + [dma((6,))] * 2
+        + [each] * 6
+        + [dma((holders,))] * 2
+        + [dma((5,))] * 2
         + [dma((3,))],
         compiler_params=pltpu.CompilerParams(
             collective_id=0, has_side_effects=True, vmem_limit_bytes=56 * 2**20

time: 169 us -> 170 us (level)
  no operation moved by 1% of the time
where the time goes in v4:
time: 170 us
  Pallas kernels  168 us (99%)
    pallas_call x1, Pallas kernels, body(): pl.pallas_call(functools.partial(layer_kernel, n), out_shape=jax.ShapeDty...  168 us

profile of v4, /device:TPU:1, one launch (start us, length us, event | category | flops | bytes accessed | tf_op | source)
XLA Modules:
  0.0 169.7 jit_solution(2959715031465580884)
XLA Ops:
  0.0 168.2 %layer.1 = bf16[2,64,128]{2,1,0:T(8,128)(2,1)} custom-call(bf16[128,256]{1,0:T(8,128)(2,1)} %q_ref.1, bf16[128,256]{1,0:T(8,128)(2,1)} %k_ref.1, bf16[128,256]{1,0:T(8,128)(2,1)} %v_ref.1, f32[2]{0:T(128)} %rate_ref.1, bf16[64,192]{1,0:T(8,128)(2,1)} %res_ref.1, bf16[192,256]{1,0:T(8,128)(2,1)} %bitcast.7, s32[2,64]{1,0:T(2,128)} %bitcast.8, ...), custom_call_target="tpu_custom_call" | custom-call | tf_op jit(solution)/shard_map/layer/pallas_call | solution.py:589
  168.2 0.7 slice_bitcast_fusion.1
  169.0 0.7 pad_maximum_fusion

commit v5 on v4

--- a/solution.py
+++ b/solution.py
@@ -60,6 +60,8 @@
     earlier,
     streams,
     turned_out,
+    terms,
+    other_terms,
     back,
     home,
     last,
@@ -133,14 +135,14 @@
             peer = along(way, steps)
             pl.semaphore_signal(barrier, inc=1, device_id={"ctx": peer}, device_id_type=MESH)
 
-    holders = 2 * n
+    pl.semaphore_signal(barrier, inc=1, device_id={"exp": partner}, device_id_type=MESH)
 
     def greet(j, carry):
-        peer = lax.rem(col + j, holders)
+        peer = 2 * lax.rem(chip + j, n) + core
         pl.semaphore_signal(barrier, inc=1, device_id={"exp": peer}, device_id_type=MESH)
         return carry
 
-    lax.fori_loop(1, holders, greet, 0)
+    lax.fori_loop(1, n, greet, 0)
 
     down_iota = lax.broadcasted_iota(jnp.int32, (count, width), 0).astype(F32)
     right_iota = lax.broadcasted_iota(jnp.int32, (count, width), 1).astype(F32)
@@ -155,7 +157,7 @@
     res_both[pl.ds(pl.multiple_of(core * own_rows, own_rows), own_rows), :] = res_ref[...]
     routes_both[core] = routes_ref[...]
     shares_both[core] = shares_ref[...]
-    pl.semaphore_wait(barrier, holders + 3)
+    pl.semaphore_wait(barrier, n + 4)
 
     rows_mine = res_both.at[pl.ds(pl.multiple_of(core * own_rows, own_rows), own_rows), :]
     rows_other = res_both.at[pl.ds(pl.multiple_of((1 - core) * own_rows, own_rows), own_rows), :]
@@ -500,47 +502,35 @@
         turned_out[f, pl.ds(0, part_width), :] = product[
             pl.ds(f * part_width, part_width), :
         ].astype(BF16)
-    owners = LANES // capacity
+    owners = LANES // (2 * capacity)
     for j in range(slots // LANES):
         for f in range(2):
             rows = dot_nt(unit(LANES, LANES), turned_out[f, :, j * LANES : (j + 1) * LANES])
-            back[pl.ds(j * owners, owners), f] = rows.astype(BF16).reshape(owners, capacity, LANES)
-
-    def homeward(j):
-        peer = lax.rem(col + j, holders)
-        sems = (back_send.at[peer], back_recv.at[col])
-        return remote(back.at[peer], home.at[col], *sems, exp=peer)
-
-    def come_home(j):
-        peer = lax.rem(col + j, holders)
-        sems = (back_send.at[peer], back_recv.at[peer])
-        return remote(home.at[peer], home.at[peer], *sems, exp=peer)
-
-    def launch_home(j, carry):
-        homeward(j).start()
-        return carry
-
-    def finish_home(j, carry):
-        come_home(j).wait_recv()
-        return carry
-
-    def home_sent(j, carry):
-        homeward(j).wait_send()
-        return carry
-
-    lax.fori_loop(1, holders, launch_home, 0)
-    home[col] = back[col]
+            rows = rows.astype(BF16).reshape(owners, 2, capacity, LANES)
+            for b in range(2):
+                terms[b, pl.ds(j * owners, owners), f] = rows[:, b]
+    swap_terms = remote(
+        terms.at[1 - core], other_terms, few_send.at[5], few_recv.at[5], exp=partner
+    )
+    swap_terms.start()
     spot = streams.at[1 - core]
     remote(spot, spot, few_send.at[4], few_recv.at[4], exp=partner).wait_recv()
     combiner = jnp.where(core == 0, combiners[0], combiners[1])
-    lax.fori_loop(1, holders, finish_home, 0)
+    swap_terms.wait_recv()
+    back[...] = (terms[core].astype(F32) + other_terms[...].astype(F32)).astype(BF16)
+    exchange(back, home, back_send, back_recv)
+
+    result = 0.0
     for f in range(2):
-        outs = home[:, f].reshape(n, 2, capacity, LANES).astype(F32)
-        outs = (outs[:, 0] + outs[:, 1]).astype(BF16).astype(F32).reshape(lanes_out, LANES)
+        outs = home[:, f].reshape(lanes_out, LANES).astype(F32)
         mixed = jnp.dot(combiner, outs, precision=BEST, preferred_element_type=F32)
-        out_ref[f] = (streams[f].astype(F32) + mixed).astype(BF16)
-
-    lax.fori_loop(1, holders, home_sent, 0)
+        value = (streams[f].astype(F32) + mixed).astype(BF16)
+        across = lax.broadcasted_iota(jnp.int32, (LANES, slice_width), 0)
+        column = lax.broadcasted_iota(jnp.int32, (LANES, slice_width), 1)
+        spread = (across + f * part_width == column) & (across < part_width)
+        result += dot_nn(value, spread.astype(F32).astype(BF16))
+    out_ref[...] = result.astype(BF16)
+
     for drain in drains:
         drain()
 
@@ -556,6 +546,7 @@
 
     lax.fori_loop(1, n, sums_sent, 0)
     swap.wait_send()
+    swap_terms.wait_send()
 
 
 def body(
@@ -588,7 +579,7 @@
     ring4, ring3, each = dma((2, half, 4)), dma((2, half, 3)), dma((n,))
     out = pl.pallas_call(
         functools.partial(layer_kernel, n),
-        out_shape=jax.ShapeDtypeStruct((2, own_rows, LANES), BF16),
+        out_shape=jax.ShapeDtypeStruct((own_rows, slice_width), BF16),
         in_specs=[on_chip] * 3
         + [pl.BlockSpec(memory_space=pltpu.SMEM)]
         + [on_chip] * 4
@@ -614,8 +605,10 @@
             vmem((heads, width, width), F32),
             vmem((2, own_rows, LANES), BF16),
             vmem((2, LANES, slots), BF16),
-            vmem((holders, 2, capacity, LANES), BF16),
-            vmem((holders, 2, capacity, LANES), BF16),
+            vmem((2, n, 2, capacity, LANES), BF16),
+            vmem((n, 2, capacity, LANES), BF16),
+            vmem((n, 2, capacity, LANES), BF16),
+            vmem((n, 2, capacity, LANES), BF16),
             vmem((own_rows, LANES), BF16),
             vmem(gate_proj.shape[1:], BF16),
             vmem(up_proj.shape[1:], BF16),
@@ -628,9 +621,8 @@
         + [ring3] * 2
         + [ring4] * 2
         + [ring3] * 2
-        + [each] * 6
-        + [dma((holders,))] * 2
-        + [dma((5,))] * 2
+        + [each] * 8
+        + [dma((6,))] * 2
         + [dma((3,))],
         compiler_params=pltpu.CompilerParams(
             collective_id=0, has_side_effects=True, vmem_limit_bytes=56 * 2**20
@@ -649,7 +641,7 @@
         up_proj,
         down_proj,
     )
-    return jnp.concatenate([out[0, :, :part_width], out[1, :, :part_width]], axis=1)
+    return out
 
 
 def solution(mesh):

time: 170 us -> 169 us (level)
  no operation moved by 1% of the time
where the time goes in v5:
time: 169 us; the launch traced here: 168 us
  Pallas kernels  167 us (99%)
    pallas_call x1, Pallas kernels, body(): pl.pallas_call(functools.partial(layer_kernel, n), out_shape=jax.ShapeDty...  167 us

profile of v5, /device:TPU:1, one launch (start us, length us, event | category | flops | bytes accessed | tf_op | source)
XLA Modules:
  0.0 168.3 jit_solution(17155659571395425703)
XLA Ops:
  0.0 166.9 %layer.1 = bf16[64,192]{1,0:T(8,128)(2,1)} custom-call(bf16[128,256]{1,0:T(8,128)(2,1)} %q_ref.1, bf16[128,256]{1,0:T(8,128)(2,1)} %k_ref.1, bf16[128,256]{1,0:T(8,128)(2,1)} %v_ref.1, f32[2]{0:T(128)} %rate_ref.1, bf16[64,192]{1,0:T(8,128)(2,1)} %res_ref.1, bf16[192,256]{1,0:T(8,128)(2,1)} %bitcast.3, s32[2,64]{1,0:T(2,128)} %bitcast.4, s32[2,64]{1,0:T(2,128)} %bitcast.5, ...), custom_call_target="tpu_custom_call" | custom-call | tf_op jit(solution)/shard_map/layer/pallas_call | solution.py:580
  166.9 1.4 copy.13
